TPU v7x, 32 devices: a whole 2x2x4 slice. The times are simulated.
32 devices in a mesh: row: 2 (over x), col: 16 (over z, y, core).
Axes of the slice: x: 2, y: 2, z: 4, core: 2. Of those that a mesh axis runs over, the one named last changes fastest.
Arguments:
- pair_state: bfloat16 [256, 256, 256], P('row', 'col'), may hold values from -6 to 6
- residue_mask: int32 [256], replicated, may hold values 0 or 1
- chain_ids: int32 [256], replicated, may hold values from 0 to 3, never falling along the last dimension, each value on 1 to 128 neighbouring positions
- gain_transition: float32 [256], replicated, may hold values from 0.1 to 1.9
- hidden_weight: bfloat16 [256, 1024], replicated, may hold values from -0.375 to 0.375
- out_weight: bfloat16 [1024, 256], replicated, may hold values from -0.1875 to 0.1875
- gain_attention: float32 [256], replicated, may hold values from 0.1 to 1.9
- query_weight: bfloat16 [256, 256], replicated, may hold values from -4 to 4
- key_weight: bfloat16 [256, 256], replicated, may hold values from -4 to 4
- value_weight: bfloat16 [256, 256], replicated, may hold values from -0.375 to 0.375
- gate_weight: bfloat16 [256, 256], replicated, may hold values from -0.375 to 0.375
- bias_weight: bfloat16 [256, 8], replicated, may hold values from -0.375 to 0.375
- chain_weight: float32 [8], replicated, may hold values from -2 to 2
- output_weight: bfloat16 [256, 256], replicated, may hold values from -4 to 4
Outputs:
- symmetric_pair: bfloat16 [256, 256, 256], P('row', 'col')
All inputs are finite; a program needn't handle non-finite values.
Results may differ from a plain program's by a relative error of at most 0.004.
The roundings to bfloat16 on the way count: a program that leaves them out, or rounds other values in their place, can miss the bound.
Values may be sent and summed in bfloat16 or wider, within the bound.
A program may use at most 128 MiB of HBM per device.

v0:
```python
import math

import jax
import jax.numpy as jnp
from jax import lax
from jax.sharding import PartitionSpec as P

mask_penalty = 1000000000.0
norm_epsilon = 1e-05


def normalize(values, gain):
    center = values - jnp.mean(values, axis=-1, keepdims=True)
    variance = jnp.mean(center * center, axis=-1, keepdims=True)
    return center * lax.rsqrt(variance + norm_epsilon) * gain


def mirror(tile):
    tile_rows, tile_cols, channels = tile.shape
    col_count = lax.axis_size("col")
    row_count = lax.axis_size("row")
    col_ratio = col_count // row_count
    piece_len = tile_cols * tile_cols // col_count
    sectioned = tile.reshape(col_ratio, col_count, piece_len, channels)
    sectioned = lax.all_to_all(sectioned, "col", split_axis=1, concat_axis=1, tiled=True)
    sectioned = sectioned.reshape(col_ratio, row_count, col_ratio, piece_len, channels)
    sectioned = lax.all_to_all(sectioned, "row", split_axis=1, concat_axis=1, tiled=True)
    sectioned = jnp.transpose(sectioned, (1, 0, 2, 3, 4)).reshape(
        col_count, col_ratio, piece_len, channels
    )
    sectioned = lax.all_to_all(sectioned, "col", split_axis=0, concat_axis=0, tiled=True)
    sectioned = jnp.transpose(sectioned, (1, 0, 2, 3)).reshape(
        col_ratio, tile_cols, tile_cols, channels
    )
    return jnp.transpose(sectioned, (0, 2, 1, 3)).reshape(tile_rows, tile_cols, channels)


def attend(query_part, gate_part, key_part, value_part, bias_part, head_count, output_weight):
    query_total = query_part.shape[0]
    key_total = key_part.shape[0]
    head_dim = query_part.shape[1] // head_count
    score_scale = 1.0 / math.sqrt(head_dim)
    query_heads = query_part.reshape(query_total, head_count, head_dim)
    key_heads = key_part.reshape(key_total, head_count, head_dim)
    value_heads = value_part.reshape(key_total, head_count, head_dim)
    scores = (
        jnp.einsum("jhd,khd->hjk", query_heads, key_heads, preferred_element_type=jnp.float32)
        * score_scale
        + bias_part
    )
    row_max = jnp.max(scores, axis=-1, keepdims=True)
    exponent = jnp.exp(scores - row_max)
    attn_weights = (exponent / jnp.sum(exponent, axis=-1, keepdims=True)).astype(jnp.bfloat16)
    mixture = jnp.einsum(
        "hjk,khd->jhd", attn_weights, value_heads, preferred_element_type=jnp.float32
    )
    gated = (gate_part * mixture.reshape(query_total, head_count * head_dim)).astype(jnp.bfloat16)
    return jnp.dot(gated, output_weight, preferred_element_type=jnp.float32).astype(jnp.bfloat16)


def mirror_layout(
    normed_tile,
    bias_tile,
    chain_ids,
    penalty,
    chain_weight,
    query_weight,
    key_weight,
    value_weight,
    gate_weight,
    output_weight,
):
    tile_rows, tile_cols, channels = normed_tile.shape
    head_count = bias_tile.shape[0]
    row_start = lax.axis_index("row") * tile_rows
    flat_tile = normed_tile.reshape(tile_rows * tile_cols, channels)
    key_tile = (
        jnp.dot(flat_tile, key_weight, preferred_element_type=jnp.float32)
        .astype(jnp.bfloat16)
        .reshape(tile_rows, tile_cols, -1)
    )
    value_tile = (
        jnp.dot(flat_tile, value_weight, preferred_element_type=jnp.float32)
        .astype(jnp.bfloat16)
        .reshape(tile_rows, tile_cols, -1)
    )
    key_all, value_all = (
        lax.all_gather(key_tile, "row", axis=0, tiled=True),
        lax.all_gather(value_tile, "row", axis=0, tiled=True),
    )
    bias_rows = lax.all_gather(bias_tile, "col", axis=2, tiled=True)
    chain_rows = lax.dynamic_slice_in_dim(chain_ids, row_start, tile_rows, 0)
    same_chain = (chain_rows[:, None] == chain_ids[None, :]).astype(jnp.float32)
    bias_full = (
        bias_rows.astype(jnp.float32)
        + chain_weight[:, None, None] * same_chain[None]
        - penalty[None, None, :]
    )
    query_tile = (
        jnp.dot(flat_tile, query_weight, preferred_element_type=jnp.float32)
        .astype(jnp.bfloat16)
        .reshape(tile_rows, tile_cols, -1)
    )
    gate_tile = jax.nn.sigmoid(
        jnp.dot(flat_tile, gate_weight, preferred_element_type=jnp.float32)
    ).reshape(tile_rows, tile_cols, -1)

    def one_column(position):
        query_part = lax.dynamic_index_in_dim(query_tile, position, 1, keepdims=False)
        gate_part = lax.dynamic_index_in_dim(gate_tile, position, 1, keepdims=False)
        key_part = lax.dynamic_index_in_dim(key_all, position, 1, keepdims=False)
        value_part = lax.dynamic_index_in_dim(value_all, position, 1, keepdims=False)
        return attend(
            query_part, gate_part, key_part, value_part, bias_full, head_count, output_weight
        )

    results = lax.map(one_column, jnp.arange(tile_cols, dtype=jnp.int32))
    return jnp.transpose(results, (1, 0, 2))


def per_device(
    pair_state,
    residue_mask,
    chain_ids,
    gain_transition,
    hidden_weight,
    out_weight,
    gain_attention,
    query_weight,
    key_weight,
    value_weight,
    gate_weight,
    bias_weight,
    chain_weight,
    output_weight,
):
    tile_rows, tile_cols, channels = pair_state.shape
    head_count = chain_weight.shape[0]
    mirrored = mirror(pair_state)
    sym_tile = pair_state.astype(jnp.float32) + mirrored.astype(jnp.float32)
    flat_sym = sym_tile.reshape(tile_rows * tile_cols, channels)
    first_norm = normalize(flat_sym, gain_transition).astype(jnp.bfloat16)
    hidden_act = jax.nn.relu(
        jnp.dot(first_norm, hidden_weight, preferred_element_type=jnp.float32)
    ).astype(jnp.bfloat16)
    carried = flat_sym + jnp.dot(hidden_act, out_weight, preferred_element_type=jnp.float32)
    normed = normalize(carried, gain_attention).astype(jnp.bfloat16)
    bias_tile = (
        jnp.einsum("pd,dh->hp", normed, bias_weight, preferred_element_type=jnp.float32)
        .astype(jnp.bfloat16)
        .reshape(head_count, tile_rows, tile_cols)
    )
    penalty = mask_penalty * (1 - residue_mask).astype(jnp.float32)
    normed_tile = normed.reshape(tile_rows, tile_cols, channels)
    arguments = (
        normed_tile,
        bias_tile,
        chain_ids,
        penalty,
        chain_weight,
        query_weight,
        key_weight,
        value_weight,
        gate_weight,
        output_weight,
    )
    own_update = mirror_layout(*arguments)
    other_update = mirror(own_update)
    total = (
        2.0 * carried.reshape(tile_rows, tile_cols, channels)
        + own_update.astype(jnp.float32)
        + other_update.astype(jnp.float32)
    )
    return total.astype(jnp.bfloat16)


def solution(mesh):
    placed = (
        P("row", "col", None),
        P(),
        P(),
        P(),
        P(),
        P(),
        P(),
        P(),
        P(),
        P(),
        P(),
        P(),
        P(),
        P(),
    )
    return jax.shard_map(
        per_device, mesh=mesh, in_specs=placed, out_specs=P("row", "col", None), check_vma=False
    )
```

profile of v0, /device:TPU:0, one launch (start us, length us, event | category | flops | bytes accessed | tf_op | source)
XLA Modules:
  0.0 411.8 jit_solution(164429025150817650)
XLA Ops:
  6.5 1.4 copy.40
  7.9 31.9 %all_to_all.30 = bf16[8,16,16,256]{3,2,0,1:T(8,128)(2,1)S(1)} all-to-all(bf16[8,16,16,256]{3,2,0,1:T(8,128)(2,1)S(1)} %copy.40), channel_id=1, replica_groups=mesh['row'=2,'col'=16] {'col'}, dimensions={1} | all-to-all | bytes 2097152 | tf_op jit(solution)/shard_map/all_to_all | solution.py:25
  39.9 17.5 %all_to_all.31 = bf16[8,2,8,16,256]{4,3,2,0,1:T(8,128)(2,1)S(1)} all-to-all(bf16[8,2,8,16,256]{4,3,2,0,1:T(8,128)(2,1)S(1)} %copy.41), channel_id=1, replica_groups=mesh['row'=2,'col'=16] {'row'}, dimensions={1} | all-to-all | bytes 2097152 | tf_op jit(solution)/shard_map/all_to_all | solution.py:27
  57.4 28.9 %all_to_all.32 = bf16[16,8,16,256]{3,2,1,0:T(8,128)(2,1)S(1)} all-to-all(bf16[16,8,16,256]{3,2,1,0:T(8,128)(2,1)S(1)} %bitcast.107), channel_id=1, replica_groups=mesh['row'=2,'col'=16] {'col'}, dimensions={0} | all-to-all | bytes 2097152 | tf_op jit(solution)/shard_map/all_to_all | solution.py:31
  87.6 1.3 fusion.18
  89.8 1.7 fusion.16
  91.4 5.0 %fusion.20 = (f32[2048]{0:T(1024)S(1)}, f32[2048,256]{1,0:T(8,128)}) fusion(f32[2048,256]{1,0:T(8,128)S(1)} %bitcast.101, bf16[1024,256]{1,0:T(8,128)(2,1)S(1)} %copy-done, bf16[2048,256]{1,0:T(8,128)(2,1)} %fusion.16, bf16[256,1024]{1,0:T(8,128)(2,1)S(1)} %copy-done.15), kind=kOutput, calls=%fused_computation.50 | convolution fusion | flops 2152724480 | bytes 6299648 | tf_op jit(solution)/shard_map/dot_general | solution.py:146
  96.5 2.4 multiply_reduce_fusion
  98.9 1.7 broadcast_multiply_fusion
  101.0 1.7 copy.43
  103.3 1.7 copy.44
  106.0 22.5 %all_gather.11 = bf16[8,128,256]{1,0,2:T(8,128)(2,1)S(1)} all-gather(bf16[8,128,16]{1,0,2:T(8,128)(2,1)S(1)} %copy.45), channel_id=1, replica_groups=mesh['row'=2,'col'=16] {'col'}, dimensions={2}, use_global_device_ids=true | all-gather | bytes 557056 | tf_op jit(solution)/shard_map/all_gather | solution.py:91
  128.5 1.3 add_subtract_fusion
  129.8 1.6 copy.48
  131.4 1.4 convolution_convert_fusion.2
  132.8 2.7 copy.47
  135.5 2.1 fusion.11
  137.6 32.4 %all-gather.5.cloned.1.call-done = bf16[256,16,256]{0,2,1:T(8,128)(2,1)} async-done(((bf16[128,16,256]{0,2,1:T(8,128)(2,1)}), bf16[256,16,256]{0,2,1:T(8,128)(2,1)}) %all-gather.5.cloned.1.call-update) | async-done | bytes 2097168 | tf_op jit(solution)/shard_map/all_gather | solution.py:88
  170.0 152.1 %while.10 = (s32[]{:T(128)}, bf16[16,128,256]{2,1,0:T(8,128)(2,1)}, s32[16]{0:T(128)S(1)}, f32[128,16,256]{2,1,0:T(8,128)}, bf16[256,16,256]{0,2,1:T(8,128)(2,1)...) while((s32[]{:T(128)}, bf16[16,128,256]{2,1,0:T(8,128)(2,1)}, ...), condition=%wide.region_7.8_spmd, body=%wide.region_4.7_spmd.sunk | while | flops 52266500 | bytes 6431407 | solution.py:117
  172.7 1.0 constant_dynamic-slice_fusion.7
  175.3 1.9 fusion.62
  177.2 1.3 constant_dynamic-slice_fusion.9
  182.2 1.0 constant_dynamic-slice_fusion.7
  184.8 1.9 fusion.62
  186.7 1.3 constant_dynamic-slice_fusion.9
  194.3 1.9 fusion.62
  196.2 1.3 constant_dynamic-slice_fusion.9
  201.3 1.0 constant_dynamic-slice_fusion.7
  203.8 1.9 fusion.62
  205.7 1.3 constant_dynamic-slice_fusion.9
  213.3 1.9 fusion.62
  215.2 1.3 constant_dynamic-slice_fusion.9
  222.8 1.9 fusion.62
  224.7 1.3 constant_dynamic-slice_fusion.9
  232.3 1.9 fusion.62
  234.2 1.3 constant_dynamic-slice_fusion.9
  241.8 1.9 fusion.62
  243.7 1.3 constant_dynamic-slice_fusion.9
  251.4 1.9 fusion.62
  253.3 1.3 constant_dynamic-slice_fusion.9
  260.9 1.9 fusion.62
  262.8 1.3 constant_dynamic-slice_fusion.9
  270.4 1.9 fusion.62
  272.3 1.3 constant_dynamic-slice_fusion.9
  279.9 1.9 fusion.62
  281.8 1.3 constant_dynamic-slice_fusion.9
  286.8 1.0 constant_dynamic-slice_fusion.7
  289.4 1.9 fusion.62
  291.3 1.3 constant_dynamic-slice_fusion.9
  296.3 1.0 constant_dynamic-slice_fusion.7
  298.9 1.9 fusion.62
  300.8 1.3 constant_dynamic-slice_fusion.9
  305.8 1.0 constant_dynamic-slice_fusion.7
  308.4 1.9 fusion.62
  310.3 1.3 constant_dynamic-slice_fusion.9
  315.3 1.0 constant_dynamic-slice_fusion.7
  317.9 1.9 fusion.62
  319.8 1.3 constant_dynamic-slice_fusion.9
  322.1 1.8 copy.50
  323.9 30.1 %all_to_all.33 = bf16[8,16,16,256]{3,2,0,1:T(8,128)(2,1)S(1)} all-to-all(bf16[8,16,16,256]{3,2,0,1:T(8,128)(2,1)S(1)} %copy.50), channel_id=1, replica_groups=mesh['row'=2,'col'=16] {'col'}, dimensions={1} | all-to-all | bytes 2097152 | tf_op jit(solution)/shard_map/all_to_all | solution.py:25
  354.5 17.5 %all_to_all.34 = bf16[8,2,8,16,256]{4,0,3,2,1:T(8,128)(2,1)S(1)} all-to-all(bf16[8,2,8,16,256]{4,0,3,2,1:T(8,128)(2,1)S(1)} %copy.51), channel_id=1, replica_groups=mesh['row'=2,'col'=16] {'row'}, dimensions={1} | all-to-all | bytes 2097152 | tf_op jit(solution)/shard_map/all_to_all | solution.py:27
  372.1 28.9 %all_to_all.35 = bf16[16,8,16,256]{3,2,1,0:T(8,128)(2,1)S(1)} all-to-all(bf16[16,8,16,256]{3,2,1,0:T(8,128)(2,1)S(1)} %bitcast.109), channel_id=1, replica_groups=mesh['row'=2,'col'=16] {'col'}, dimensions={0} | all-to-all | bytes 2097152 | tf_op jit(solution)/shard_map/all_to_all | solution.py:31
  401.4 1.2 copy.53
  403.2 1.8 fusion.13
  (182 shorter events, 65.3 us)
Async XLA Ops:
  6.5 84.9 %copy-start = (bf16[1024,256]{1,0:T(8,128)(2,1)S(1)}, bf16[1024,256]{1,0:T(8,128)(2,1)}, u32[]{:S(2)}) copy-start(bf16[1024,256]{1,0:T(8,128)(2,1)} %param.21) | copy-start | bytes 1572868
  6.5 131.1 %all-gather.3.cloned.1.call-start = ((), (), s32[]{:S(2)}) async-start(), calls=%async_computation.6 | async-start | bytes 3145728 | tf_op jit(solution)/shard_map/all_gather | solution.py:89
  86.3 1.2 copy-start.3
  88.9 0.9 copy-start.10
  89.6 1.8 copy-start.15
  96.5 2.4 copy-start.2
  96.5 2.4 copy-start.13
  98.9 1.7 copy-start.6
  101.0 1.8 copy-start.7
  102.7 67.3 %all-gather.5.cloned.1.call-start = ((), (), s32[]{:S(2)}) async-start(), calls=%async_computation.7 | async-start | bytes 3145728 | tf_op jit(solution)/shard_map/all_gather | solution.py:88
  103.2 1.8 copy-start.11
  103.2 1.9 copy-start.12
  103.2 2.0 copy-start.9
  105.0 23.5 %copy-start.14 = (f32[8]{0:T(128)S(1)}, f32[8]{0:T(128)}, u32[]{:S(2)}) copy-start(f32[8]{0:T(128)} %param.28) | copy-start | bytes 100
  106.0 25.4 %copy-start.8 = (bf16[256,256]{1,0:T(8,128)(2,1)S(1)}, bf16[256,256]{1,0:T(8,128)(2,1)}, u32[]{:S(2)}) copy-start(bf16[256,256]{1,0:T(8,128)(2,1)} %param.23) | copy-start | bytes 393220
  131.4 4.1 %copy-start.16 = (bf16[256,256]{1,0:T(8,128)(2,1)S(1)}, bf16[256,256]{1,0:T(8,128)(2,1)}, u32[]{:S(2)}) copy-start(bf16[256,256]{1,0:T(8,128)(2,1)} %param.26) | copy-start | bytes 393220
  135.5 34.5 %copy-start.5 = (bf16[256,256]{1,0:T(8,128)(2,1)S(1)}, bf16[256,256]{1,0:T(8,128)(2,1)}, u32[]{:S(2)}) copy-start(bf16[256,256]{1,0:T(8,128)(2,1)} %param.29) | copy-start | bytes 393220
  401.4 1.6 copy-start.1
  401.4 1.9 copy-start.4
Sparse Core Ops, SparseCore 0:
  102.8 32.4 all-gather.2
  136.9 33.0 all-gather.4
where the time goes:
time: 415 us; the launch traced here: 412 us
  blocking collectives  177 us (43%)
  local copies, waits for them, and re-layouts  78.1 us (19%)
  matrix products  59.1 us (14%)
  loops' own time  33.7 us (8%)
  waiting for transfers between devices  32.4 us (8%)
  other arithmetic  17.6 us (4%)
  between operations  13.7 us (3%)
    all_to_all x2, blocking collectives, mirror(): lax.all_to_all(sectioned, 'col', split_axis=1, concat_axis=1, tiled=True)  62 us
    all_to_all x2, blocking collectives, mirror(): lax.all_to_all(sectioned, 'col', split_axis=0, concat_axis=0, tiled=True)  57.9 us
    all_to_all x2, blocking collectives, mirror(): lax.all_to_all(sectioned, 'row', split_axis=1, concat_axis=1, tiled=True)  34.9 us
    another operation x1, loops' own time, mirror_layout(): results = lax.map(one_column, jnp.arange(tile_cols, dtype=jnp.int32))  33.7 us
    all_gather x1, waiting for transfers between devices, mirror_layout(): lax.all_gather(key_tile, 'row', axis=0, tiled=True)  32.4 us
    dot_general x16, matrix products, attend(): jnp.einsum('hjk,khd->jhd', attn_weights, value_heads, preferred_element_t...  30.4 us
    dynamic_slice x32, local copies, waits for them, and re-layouts, one_column(): gate_part = lax.dynamic_index_in_dim(gate_tile, position, 1, keepdims=False)  23 us
    all_gather x1, blocking collectives, mirror_layout(): bias_rows = lax.all_gather(bias_tile, 'col', axis=2, tiled=True)  22.5 us
  transfers between devices with their start and end apart: 2, of which 1 were waited for; matrix products, arithmetic and copies ran while one was open for 3% of the time, Pallas kernels for 0%

commit v1 on v0

--- a/solution.py
+++ b/solution.py
@@ -1,9 +1,15 @@
+import functools
 import math
 
 import jax
 import jax.numpy as jnp
 from jax import lax
+from jax.experimental import pallas as pl
+from jax.experimental.pallas import tpu as pltpu
 from jax.sharding import PartitionSpec as P
+
+MESH = pl.DeviceIdType.MESH
+VMEM_LIMIT = 60 * 1024 * 1024
 
 mask_penalty = 1000000000.0
 norm_epsilon = 1e-05
@@ -118,7 +124,7 @@
     return jnp.transpose(results, (1, 0, 2))
 
 
-def per_device(
+def tile_layout(
     pair_state,
     residue_mask,
     chain_ids,
@@ -174,6 +180,435 @@
     return total.astype(jnp.bfloat16)
 
 
+def greet_all(row_count, col_count):
+    device_total = row_count * col_count
+    me = lax.axis_index("col") * row_count + lax.axis_index("row")
+    barrier = pltpu.get_barrier_semaphore()
+
+    def greet(step, carry):
+        peer = lax.rem(me + step, device_total)
+        pl.semaphore_signal(
+            barrier,
+            inc=1,
+            device_id=(lax.rem(peer, row_count), peer // row_count),
+            device_id_type=MESH,
+        )
+        return carry
+
+    lax.fori_loop(1, device_total, greet, 0)
+    pl.semaphore_wait(barrier, device_total - 1)
+
+
+def transition_kernel(
+    row_count,
+    col_count,
+    tile_ref,
+    turned_ref,
+    gain_transition_ref,
+    hidden_weight_ref,
+    out_weight_ref,
+    gain_attention_ref,
+    bias_weight_ref,
+    carried_ref,
+    normed_ref,
+    bias_ref,
+    row_buf,
+    col_buf,
+    row_send,
+    row_recv,
+    col_send,
+    col_recv,
+    bias_send,
+    bias_recv,
+):
+    tile_rows, tile_cols, channels = tile_ref.shape
+    own = tile_cols // row_count
+    groups = tile_rows // own
+    device_total = row_count * col_count
+    row_id, col_id = lax.axis_index("row"), lax.axis_index("col")
+    me = col_id * row_count + row_id
+    greet_all(row_count, col_count)
+
+    def row_copy(group):
+        target = row_id * groups + group
+        source = tile_ref.at[pl.ds(group * own, own)]
+        landing = row_buf.at[:, pl.ds(pl.multiple_of(col_id * tile_cols, tile_cols), tile_cols), :]
+        return target, source, landing
+
+    def row_remote(group):
+        target, source, landing = row_copy(group)
+        return pltpu.make_async_remote_copy(
+            src_ref=source,
+            dst_ref=landing,
+            send_sem=row_send.at[group],
+            recv_sem=row_recv.at[col_id],
+            device_id=(lax.rem(target, row_count), target // row_count),
+            device_id_type=MESH,
+        )
+
+    def row_local(group):
+        target, source, landing = row_copy(group)
+        return pltpu.make_async_copy(source, landing, row_recv.at[col_id])
+
+    def col_remote(other):
+        return pltpu.make_async_remote_copy(
+            src_ref=turned_ref.at[pl.ds(other * own, own)],
+            dst_ref=col_buf.at[
+                :, pl.ds(pl.multiple_of(row_id * tile_rows, tile_rows), tile_rows), :
+            ],
+            send_sem=col_send.at[other],
+            recv_sem=col_recv.at[row_id],
+            device_id=(other, col_id),
+            device_id_type=MESH,
+        )
+
+    def start_row(step, carry):
+        group = lax.rem(step + me, groups)
+        target = row_id * groups + group
+
+        @pl.when(target != me)
+        def _():
+            row_remote(group).start()
+
+        @pl.when(target == me)
+        def _():
+            row_local(group).start()
+
+        return carry
+
+    lax.fori_loop(0, groups, start_row, 0)
+
+    def start_col(step, carry):
+        col_remote(lax.rem(row_id + step, row_count)).start()
+        return carry
+
+    lax.fori_loop(1, row_count, start_col, 0)
+    own_col = pltpu.make_async_copy(
+        turned_ref.at[pl.ds(row_id * own, own)],
+        col_buf.at[:, pl.ds(pl.multiple_of(row_id * tile_rows, tile_rows), tile_rows), :],
+        col_recv.at[row_id],
+    )
+    own_col.start()
+
+    def wait_row(other, carry):
+        landed = row_buf.at[:, pl.ds(pl.multiple_of(other * tile_cols, tile_cols), tile_cols), :]
+        pltpu.make_async_copy(landed, landed, row_recv.at[other]).wait()
+        return carry
+
+    lax.fori_loop(0, col_count, wait_row, 0)
+
+    def wait_col(other, carry):
+        landed = col_buf.at[:, pl.ds(pl.multiple_of(other * tile_rows, tile_rows), tile_rows), :]
+        pltpu.make_async_copy(landed, landed, col_recv.at[other]).wait()
+        return carry
+
+    lax.fori_loop(0, row_count, wait_col, 0)
+
+    def one_row(position, carry):
+        sym_row = row_buf[position].astype(jnp.float32) + col_buf[position].astype(jnp.float32)
+        first_norm = normalize(sym_row, gain_transition_ref[...]).astype(jnp.bfloat16)
+        hidden_act = jax.nn.relu(
+            jnp.dot(first_norm, hidden_weight_ref[...], preferred_element_type=jnp.float32)
+        ).astype(jnp.bfloat16)
+        carried = sym_row + jnp.dot(
+            hidden_act, out_weight_ref[...], preferred_element_type=jnp.float32
+        )
+        carried_ref[position] = carried
+        normed = normalize(carried, gain_attention_ref[...]).astype(jnp.bfloat16)
+        normed_ref[position] = normed
+        bias_ref[me * own + position] = lax.dot_general(
+            bias_weight_ref[...],
+            normed,
+            (((1,), (1,)), ((), ())),
+            preferred_element_type=jnp.float32,
+        ).astype(jnp.bfloat16)
+        return carry
+
+    lax.fori_loop(0, own, one_row, 0)
+
+    def bias_remote(peer):
+        return pltpu.make_async_remote_copy(
+            src_ref=bias_ref.at[pl.ds(me * own, own)],
+            dst_ref=bias_ref.at[pl.ds(me * own, own)],
+            send_sem=bias_send.at[peer],
+            recv_sem=bias_recv.at[me],
+            device_id=(lax.rem(peer, row_count), peer // row_count),
+            device_id_type=MESH,
+        )
+
+    def start_bias(step, carry):
+        bias_remote(lax.rem(me + step, device_total)).start()
+        return carry
+
+    lax.fori_loop(1, device_total, start_bias, 0)
+
+    def wait_bias(step, carry):
+        peer = lax.rem(me + step, device_total)
+        landed = bias_ref.at[pl.ds(peer * own, own)]
+        pltpu.make_async_copy(landed, landed, bias_recv.at[peer]).wait()
+        bias_remote(peer).wait_send()
+        return carry
+
+    lax.fori_loop(1, device_total, wait_bias, 0)
+
+    def finish_row(group, carry):
+        @pl.when(row_id * groups + group != me)
+        def _():
+            row_remote(group).wait_send()
+
+        return carry
+
+    lax.fori_loop(0, groups, finish_row, 0)
+
+    def finish_col(step, carry):
+        col_remote(lax.rem(row_id + step, row_count)).wait_send()
+        return carry
+
+    lax.fori_loop(1, row_count, finish_col, 0)
+
+
+def attention_kernel(
+    row_count,
+    col_count,
+    carried_ref,
+    normed_ref,
+    bias_ref,
+    query_weight_ref,
+    key_weight_ref,
+    value_weight_ref,
+    gate_weight_ref,
+    output_weight_ref,
+    out_ref,
+    total,
+    update_buf,
+    recv_buf,
+    turned,
+    sum_buf,
+    update_send,
+    update_recv,
+    sum_send,
+    sum_recv,
+):
+    own, length, channels = normed_ref.shape
+    head_count = bias_ref.shape[0]
+    head_dim = query_weight_ref.shape[1] // head_count
+    score_scale = 1.0 / math.sqrt(head_dim)
+    tile_rows = length // row_count
+    device_total = row_count * col_count
+    row_id, col_id = lax.axis_index("row"), lax.axis_index("col")
+    me = col_id * row_count + row_id
+    greet_all(row_count, col_count)
+
+    def update_remote(position, peer):
+        return pltpu.make_async_remote_copy(
+            src_ref=update_buf.at[position, peer],
+            dst_ref=recv_buf.at[me * own + position],
+            send_sem=update_send.at[peer],
+            recv_sem=update_recv.at[me],
+            device_id=(lax.rem(peer, row_count), peer // row_count),
+            device_id_type=MESH,
+        )
+
+    head_of_lane = lax.broadcasted_iota(jnp.int32, (1, channels), 1) // head_dim
+
+    def one_row(position, carry):
+        normed = normed_ref[position]
+
+        def project(weight_ref):
+            return jnp.dot(normed, weight_ref[...], preferred_element_type=jnp.float32)
+
+        queries = project(query_weight_ref).astype(jnp.bfloat16)
+        keys_turned = project(key_weight_ref).astype(jnp.bfloat16).T
+        values = project(value_weight_ref).astype(jnp.bfloat16)
+        gates = jax.nn.sigmoid(project(gate_weight_ref))
+        mixture = jnp.zeros((length, channels), jnp.float32)
+        for head in range(head_count):
+            chosen = (head_of_lane == head).astype(jnp.bfloat16)
+            scores = (
+                jnp.dot(queries * chosen, keys_turned, preferred_element_type=jnp.float32)
+                * score_scale
+                + bias_ref[head]
+            )
+            row_max = jnp.max(scores, axis=-1, keepdims=True)
+            exponent = jnp.exp(scores - row_max)
+            attn_weights = (
+                exponent * (1.0 / jnp.sum(exponent, axis=-1, keepdims=True))
+            ).astype(jnp.bfloat16)
+            mixture = mixture + jnp.dot(
+                attn_weights, values * chosen, preferred_element_type=jnp.float32
+            )
+        gated = (gates * mixture).astype(jnp.bfloat16)
+        update = jnp.dot(gated, output_weight_ref[...], preferred_element_type=jnp.float32)
+        update = update.reshape(device_total, own, channels).astype(jnp.bfloat16)
+        update_buf[position] = update
+        recv_buf[me * own + position] = update_buf[position, me]
+        total[position] = 2.0 * carried_ref[position] + update.astype(jnp.float32).reshape(
+            length, channels
+        )
+
+        def send(step, inner):
+            update_remote(position, lax.rem(me + step, device_total)).start()
+            return inner
+
+        lax.fori_loop(1, device_total, send, 0)
+        return carry
+
+    lax.fori_loop(0, own, one_row, 0)
+    for position in range(own):
+        turned[:, position, :] = total[position]
+
+    def wait_update(step, carry):
+        peer = lax.rem(me + step, device_total)
+        landed = recv_buf.at[pl.ds(peer * own, own)]
+        pltpu.make_async_copy(landed, landed, update_recv.at[peer]).wait()
+        pltpu.make_async_copy(landed, landed, update_send.at[peer]).wait()
+        return carry
+
+    lax.fori_loop(1, device_total, wait_update, 0)
+
+    def sum_remote(other):
+        return pltpu.make_async_remote_copy(
+            src_ref=sum_buf.at[other],
+            dst_ref=out_ref.at[row_id],
+            send_sem=sum_send.at[other],
+            recv_sem=sum_recv.at[row_id],
+            device_id=(other, col_id),
+            device_id_type=MESH,
+        )
+
+    def sum_rows(other, target_ref):
+        def one_block(block, carry):
+            rows = pl.ds(other * tile_rows + block * own, own)
+            summed = turned[rows] + recv_buf[rows].astype(jnp.float32)
+            target_ref[other, pl.ds(block * own, own)] = summed.astype(jnp.bfloat16)
+            return carry
+
+        lax.fori_loop(0, tile_rows // own, one_block, 0)
+
+    def send_sum(step, carry):
+        other = lax.rem(row_id + step, row_count)
+        sum_rows(other, sum_buf)
+        sum_remote(other).start()
+        return carry
+
+    lax.fori_loop(1, row_count, send_sum, 0)
+    sum_rows(row_id, out_ref)
+
+    def wait_sum(step, carry):
+        other = lax.rem(row_id + step, row_count)
+        landed = out_ref.at[other]
+        pltpu.make_async_copy(landed, landed, sum_recv.at[other]).wait()
+        sum_remote(other).wait_send()
+        return carry
+
+    lax.fori_loop(1, row_count, wait_sum, 0)
+
+
+def owned_columns(
+    pair_state,
+    residue_mask,
+    chain_ids,
+    gain_transition,
+    hidden_weight,
+    out_weight,
+    gain_attention,
+    query_weight,
+    key_weight,
+    value_weight,
+    gate_weight,
+    bias_weight,
+    chain_weight,
+    output_weight,
+):
+    tile_rows, tile_cols, channels = pair_state.shape
+    row_count, col_count = lax.axis_size("row"), lax.axis_size("col")
+    device_total = row_count * col_count
+    head_count = chain_weight.shape[0]
+    length = tile_rows * row_count
+    own = tile_cols // row_count
+    in_vmem = pl.BlockSpec(memory_space=pltpu.VMEM)
+    dma = pltpu.SemaphoreType.DMA
+    carried, normed, bias_rows = pl.pallas_call(
+        functools.partial(transition_kernel, row_count, col_count),
+        out_shape=(
+            jax.ShapeDtypeStruct((own, length, channels), jnp.float32),
+            jax.ShapeDtypeStruct((own, length, channels), jnp.bfloat16),
+            jax.ShapeDtypeStruct((length, head_count, length), jnp.bfloat16),
+        ),
+        in_specs=[in_vmem] * 7,
+        out_specs=(in_vmem,) * 3,
+        scratch_shapes=[
+            pltpu.VMEM((own, length, channels), jnp.bfloat16),
+            pltpu.VMEM((own, length, channels), jnp.bfloat16),
+            dma((tile_rows // own,)),
+            dma((col_count,)),
+            dma((row_count,)),
+            dma((row_count,)),
+            dma((device_total,)),
+            dma((device_total,)),
+        ],
+        compiler_params=pltpu.CompilerParams(
+            collective_id=0, has_side_effects=True, vmem_limit_bytes=VMEM_LIMIT
+        ),
+        name="transition",
+    )(
+        pair_state,
+        jnp.transpose(pair_state, (1, 0, 2)),
+        gain_transition[None, :],
+        hidden_weight,
+        out_weight,
+        gain_attention[None, :],
+        bias_weight.T,
+    )
+    penalty = mask_penalty * (1 - residue_mask).astype(jnp.float32)
+    same_chain = (chain_ids[:, None] == chain_ids[None, :]).astype(jnp.float32)
+    bias_full = (
+        jnp.transpose(bias_rows, (1, 0, 2)).astype(jnp.float32)
+        + chain_weight[:, None, None] * same_chain[None]
+        - penalty[None, None, :]
+    )
+    pieces = pl.pallas_call(
+        functools.partial(attention_kernel, row_count, col_count),
+        out_shape=jax.ShapeDtypeStruct((row_count, tile_rows, own, channels), jnp.bfloat16),
+        in_specs=[in_vmem] * 8,
+        out_specs=in_vmem,
+        scratch_shapes=[
+            pltpu.VMEM((own, length, channels), jnp.float32),
+            pltpu.VMEM((own, device_total, own, channels), jnp.bfloat16),
+            pltpu.VMEM((length, own, channels), jnp.bfloat16),
+            pltpu.VMEM((length, own, channels), jnp.float32),
+            pltpu.VMEM((row_count, tile_rows, own, channels), jnp.bfloat16),
+            dma((device_total,)),
+            dma((device_total,)),
+            dma((row_count,)),
+            dma((row_count,)),
+        ],
+        compiler_params=pltpu.CompilerParams(
+            collective_id=1, has_side_effects=True, vmem_limit_bytes=VMEM_LIMIT
+        ),
+        name="attention",
+    )(
+        carried,
+        normed,
+        bias_full,
+        query_weight,
+        key_weight,
+        value_weight,
+        gate_weight,
+        output_weight,
+    )
+    return jnp.transpose(pieces, (1, 0, 2, 3)).reshape(tile_rows, tile_cols, channels)
+
+
+def per_device(pair_state, *others):
+    tile_cols = pair_state.shape[1]
+    row_count = lax.axis_size("row")
+    own = tile_cols // row_count
+    if own % 8 == 0:
+        return owned_columns(pair_state, *others)
+    return tile_layout(pair_state, *others)
+
+
 def solution(mesh):
     placed = (
         P("row", "col", None),

time: 415 us -> 143 us (0.34)
  blocking collectives: 177 us -> 0 us
  Pallas kernels: 0 us -> 133 us
  local copies, waits for them, and re-layouts: 78.1 us -> 4.81 us
  matrix products: 59.1 us -> 0 us
  loops' own time: 33.7 us -> 0 us
  waiting for transfers between devices: 32.4 us -> 0 us
  between operations: 13.7 us -> 0.03 us
  other arithmetic: 17.6 us -> 4.37 us
    all_to_all x6 -> x0, blocking collectives: 155 us -> none  [the longest x2 62 us: mirror(): lax.all_to_all(sectioned, 'col', split_axis=1, concat_axis=1, tiled=True)]
    pallas_call x0 -> x2, Pallas kernels: none -> 133 us  [the longest x1 82.2 us: owned_columns(): pl.pallas_call(functools.partial(transition_kernel, row_count, col_count)...]
    dynamic_slice x81 -> x0, local copies, waits for them, and re-layouts: 63.1 us -> none  [the longest x32 23 us: one_column(): gate_part = lax.dynamic_index_in_dim(gate_tile, position, 1, keepdims=False)]
    dot_general x54 -> x0, matrix products: 59.1 us -> none  [the longest x16 30.4 us: attend(): jnp.einsum('hjk,khd->jhd', attn_weights, value_heads, preferred_element_t...]
    another operation x1 -> x0, loops' own time: 33.7 us -> none  [mirror_layout(): results = lax.map(one_column, jnp.arange(tile_cols, dtype=jnp.int32))]
    all_gather x2 -> x0, waiting for transfers between devices: 32.4 us -> none  [the longest x1 32.4 us: mirror_layout(): lax.all_gather(key_tile, 'row', axis=0, tiled=True)]
    all_gather x1 -> x0, blocking collectives: 22.5 us -> none  [mirror_layout(): bias_rows = lax.all_gather(bias_tile, 'col', axis=2, tiled=True)]
    reshape x8 -> x1, local copies, waits for them, and re-layouts: 7.47 us -> 2.28 us  [owned_columns(): jnp.transpose(pieces, (1, 0, 2, 3)).reshape(tile_rows, tile_cols, channels)]
  transfers between devices with their start and end apart: 2 -> 0, of which waited for: 1 -> 0; matrix products, arithmetic and copies ran while one was open for 3% -> 0% of each run, Pallas kernels for 0% -> 0%
where the time goes in v1:
time: 143 us
  Pallas kernels  133 us (93%)
  local copies, waits for them, and re-layouts  4.81 us (3%)
  other arithmetic  4.37 us (3%)
    pallas_call x1, Pallas kernels, owned_columns(): pl.pallas_call(functools.partial(transition_kernel, row_count, col_count)...  82.2 us
    pallas_call x1, Pallas kernels, owned_columns(): pl.pallas_call(functools.partial(attention_kernel, row_count, col_count),...  51.2 us

profile of v1, /device:TPU:0, one launch (start us, length us, event | category | flops | bytes accessed | tf_op | source)
XLA Modules:
  0.0 142.7 jit_solution(312668868889665537)
XLA Ops:
  0.0 0.7 convert_multiply_fusion
  0.7 0.9 compare_convert_fusion
  1.5 2.5 %copy.23 = bf16[128,16,256]{2,0,1:T(8,128)(2,1)} copy(bf16[128,16,256]{2,1,0:T(8,128)(2,1)} %tile_ref.1) | data formatting | bytes 2097152 | tf_op args[0]
  4.1 0.0 copy-start
  4.1 82.2 %transition.1 = (f32[8,256,256]{2,1,0:T(8,128)}, bf16[8,256,256]{2,1,0:T(8,128)(2,1)}, bf16[256,8,256]{2,1,0:T(8,128)(2,1)}) custom-call(bf16[128,16,256]{2,1,0:T(8,128)(2,1)} %tile_ref.1, bf16[16,128,256]{2,1,0:T(8,128)(2,1)} %bitcast.15, f32[1,256]{1,0:T(1,128)} %bitcast.17, bf16[256,1024]{1,0:T(8,128)(2,1)} %hidden_weight_ref.1, ...), custom_call_target="tpu_custom_call" | custom-call | tf_op jit(solution)/shard_map/transition/pallas_call | solution.py:531
  86.3 0.0 copy-done
  86.3 2.8 %fusion.bias_ref = f32[8,256,256]{2,1,0:T(8,128)} fusion(bf16[256,8,256]{2,1,0:T(8,128)(2,1)} %get-tuple-element.10, f32[256]{0:T(256)S(1)} %convert_multiply_fusion, f32[256,256]{1,0:T(8,128)S(1)} %compare_convert_fusion, f32[8]{0:T(128)S(1)} %copy-done), kind=kLoop, calls=%fused_computation.1 | loop fusion | flops 2097152 | bytes 3408928 | tf_op jit(solution)/shard_map/sub | solution.py:566
  89.2 51.2 %attention.1 = bf16[2,128,8,256]{3,2,1,0:T(8,128)(2,1)} custom-call(f32[8,256,256]{2,1,0:T(8,128)} %get-tuple-element.8.carried_ref, bf16[8,256,256]{2,1,0:T(8,128)(2,1)} %get-tuple-element.9.normed_ref, f32[8,256,256]{2,1,0:T(8,128)} %fusion.bias_ref, bf16[256,256]{1,0:T(8,128)(2,1)} %query_weight_ref.1, bf16[256,256]{1,0:T(8,128)(2,1)} %key_weight_ref.1, ...), custom_call_target="tpu_custom_call" | custom-call | tf_op jit(solution)/shard_map/attention/pallas_call | solution.py:570
  140.4 2.3 %copy_bitcast_fusion = bf16[128,16,256]{2,1,0:T(8,128)(2,1)} fusion(bf16[2,128,8,256]{3,2,1,0:T(8,128)(2,1)} %attention.1), kind=kLoop, calls=%fused_computation.2 | loop fusion | bytes 2097152 | tf_op jit(solution)/shard_map/reshape | solution.py:600
Async XLA Ops:
  4.1 82.3 %copy-start = (f32[8]{0:T(128)S(1)}, f32[8]{0:T(128)}, u32[]{:S(2)}) copy-start(f32[8]{0:T(128)} %param.26) | copy-start | bytes 100

commit v2 on v1

--- a/solution.py
+++ b/solution.py
@@ -214,41 +214,56 @@
     bias_ref,
     row_buf,
     col_buf,
+    relay_buf,
+    relay_send,
+    relay_recv,
     row_send,
     row_recv,
     col_send,
     col_recv,
     bias_send,
     bias_recv,
+    pair_send,
+    pair_recv,
 ):
     tile_rows, tile_cols, channels = tile_ref.shape
     own = tile_cols // row_count
-    groups = tile_rows // own
-    device_total = row_count * col_count
+    span = col_count // row_count
+    chip_total = row_count * col_count // 2
     row_id, col_id = lax.axis_index("row"), lax.axis_index("col")
     me = col_id * row_count + row_id
+    side = lax.rem(col_id, 2)
+    chip = (col_id // 2) * row_count + row_id
     greet_all(row_count, col_count)
 
-    def row_copy(group):
-        target = row_id * groups + group
-        source = tile_ref.at[pl.ds(group * own, own)]
+    def relay_copy(other, slot):
+        return pltpu.make_async_remote_copy(
+            src_ref=tile_ref.at[pl.ds((slot * row_count + other) * own, own)],
+            dst_ref=relay_buf.at[row_id, slot],
+            send_sem=relay_send.at[other, slot],
+            recv_sem=relay_recv.at[row_id, slot],
+            device_id=(other, col_id),
+            device_id_type=MESH,
+        )
+
+    def start_rows(origin, slot, source):
+        target = origin * span + slot
         landing = row_buf.at[:, pl.ds(pl.multiple_of(col_id * tile_cols, tile_cols), tile_cols), :]
-        return target, source, landing
-
-    def row_remote(group):
-        target, source, landing = row_copy(group)
-        return pltpu.make_async_remote_copy(
-            src_ref=source,
-            dst_ref=landing,
-            send_sem=row_send.at[group],
-            recv_sem=row_recv.at[col_id],
-            device_id=(lax.rem(target, row_count), target // row_count),
-            device_id_type=MESH,
-        )
-
-    def row_local(group):
-        target, source, landing = row_copy(group)
-        return pltpu.make_async_copy(source, landing, row_recv.at[col_id])
+
+        @pl.when(target != col_id)
+        def _():
+            pltpu.make_async_remote_copy(
+                src_ref=source,
+                dst_ref=landing,
+                send_sem=row_send.at[origin, slot],
+                recv_sem=row_recv.at[col_id],
+                device_id=(row_id, target),
+                device_id_type=MESH,
+            ).start()
+
+        @pl.when(target == col_id)
+        def _():
+            pltpu.make_async_copy(source, landing, row_recv.at[col_id]).start()
 
     def col_remote(other):
         return pltpu.make_async_remote_copy(
@@ -262,27 +277,27 @@
             device_id_type=MESH,
         )
 
-    def start_row(step, carry):
-        group = lax.rem(step + me, groups)
-        target = row_id * groups + group
-
-        @pl.when(target != me)
-        def _():
-            row_remote(group).start()
-
-        @pl.when(target == me)
-        def _():
-            row_local(group).start()
-
-        return carry
-
-    lax.fori_loop(0, groups, start_row, 0)
-
-    def start_col(step, carry):
-        col_remote(lax.rem(row_id + step, row_count)).start()
-        return carry
-
-    lax.fori_loop(1, row_count, start_col, 0)
+    def over_rows(body):
+        def one(step, carry):
+            body(lax.rem(row_id + step, row_count))
+            return carry
+
+        lax.fori_loop(1, row_count, one, 0)
+
+    def over_slots(body):
+        def one(step, carry):
+            body(lax.rem(col_id + step, span))
+            return carry
+
+        lax.fori_loop(0, span, one, 0)
+
+    over_rows(lambda other: over_slots(lambda slot: relay_copy(other, slot).start()))
+    over_slots(
+        lambda slot: start_rows(
+            row_id, slot, tile_ref.at[pl.ds((slot * row_count + row_id) * own, own)]
+        )
+    )
+    over_rows(lambda other: col_remote(other).start())
     own_col = pltpu.make_async_copy(
         turned_ref.at[pl.ds(row_id * own, own)],
         col_buf.at[:, pl.ds(pl.multiple_of(row_id * tile_rows, tile_rows), tile_rows), :],
@@ -290,6 +305,13 @@
     )
     own_col.start()
 
+    def pass_on(origin, slot):
+        arrived = relay_buf.at[origin, slot]
+        pltpu.make_async_copy(arrived, arrived, relay_recv.at[origin, slot]).wait()
+        start_rows(origin, slot, arrived)
+
+    over_rows(lambda origin: over_slots(lambda slot: pass_on(origin, slot)))
+
     def wait_row(other, carry):
         landed = row_buf.at[:, pl.ds(pl.multiple_of(other * tile_cols, tile_cols), tile_cols), :]
         pltpu.make_async_copy(landed, landed, row_recv.at[other]).wait()
@@ -303,6 +325,20 @@
         return carry
 
     lax.fori_loop(0, row_count, wait_col, 0)
+
+    def over_chips(body):
+        def one(step, carry):
+            body(lax.rem(chip + step, chip_total))
+            return carry
+
+        lax.fori_loop(1, chip_total, one, 0)
+
+    def chip_place(other, which):
+        return lax.rem(other, row_count), (other // row_count) * 2 + which
+
+    def slab(other, which):
+        place = chip_place(other, which)
+        return bias_ref.at[pl.ds((place[1] * row_count + place[0]) * own, own)]
 
     def one_row(position, carry):
         sym_row = row_buf[position].astype(jnp.float32) + col_buf[position].astype(jnp.float32)
@@ -322,49 +358,63 @@
             (((1,), (1,)), ((), ())),
             preferred_element_type=jnp.float32,
         ).astype(jnp.bfloat16)
+        over_chips(
+            lambda other: pltpu.make_async_remote_copy(
+                src_ref=bias_ref.at[me * own + position],
+                dst_ref=bias_ref.at[me * own + position],
+                send_sem=bias_send.at[other],
+                recv_sem=bias_recv.at[chip],
+                device_id=chip_place(other, side),
+                device_id_type=MESH,
+            ).start()
+        )
         return carry
 
     lax.fori_loop(0, own, one_row, 0)
 
-    def bias_remote(peer):
+    def to_pair(other):
         return pltpu.make_async_remote_copy(
-            src_ref=bias_ref.at[pl.ds(me * own, own)],
-            dst_ref=bias_ref.at[pl.ds(me * own, own)],
-            send_sem=bias_send.at[peer],
-            recv_sem=bias_recv.at[me],
-            device_id=(lax.rem(peer, row_count), peer // row_count),
+            src_ref=slab(other, side),
+            dst_ref=slab(other, side),
+            send_sem=pair_send.at[other],
+            recv_sem=pair_recv.at[other],
+            device_id=(row_id, col_id + 1 - 2 * side),
             device_id_type=MESH,
         )
 
-    def start_bias(step, carry):
-        bias_remote(lax.rem(me + step, device_total)).start()
-        return carry
-
-    lax.fori_loop(1, device_total, start_bias, 0)
-
-    def wait_bias(step, carry):
-        peer = lax.rem(me + step, device_total)
-        landed = bias_ref.at[pl.ds(peer * own, own)]
-        pltpu.make_async_copy(landed, landed, bias_recv.at[peer]).wait()
-        bias_remote(peer).wait_send()
-        return carry
-
-    lax.fori_loop(1, device_total, wait_bias, 0)
-
-    def finish_row(group, carry):
-        @pl.when(row_id * groups + group != me)
+    to_pair(chip).start()
+
+    def hand_over(other):
+        landed = slab(other, side)
+        pltpu.make_async_copy(landed, landed, bias_recv.at[other]).wait()
+        to_pair(other).start()
+
+    over_chips(hand_over)
+
+    def close_pair(other, carry):
+        landed = slab(other, 1 - side)
+        pltpu.make_async_copy(landed, landed, pair_recv.at[other]).wait()
+        to_pair(other).wait_send()
+        return carry
+
+    lax.fori_loop(0, chip_total, close_pair, 0)
+
+    def close_chip(other):
+        sent = slab(chip, side)
+        pltpu.make_async_copy(sent, sent, bias_send.at[other]).wait()
+
+    over_chips(close_chip)
+
+    def close_rows(origin, slot):
+        @pl.when(origin * span + slot != col_id)
         def _():
-            row_remote(group).wait_send()
-
-        return carry
-
-    lax.fori_loop(0, groups, finish_row, 0)
-
-    def finish_col(step, carry):
-        col_remote(lax.rem(row_id + step, row_count)).wait_send()
-        return carry
-
-    lax.fori_loop(1, row_count, finish_col, 0)
+            sent = relay_buf.at[origin, slot]
+            pltpu.make_async_copy(sent, sent, row_send.at[origin, slot]).wait()
+
+    over_slots(lambda slot: close_rows(row_id, slot))
+    over_rows(lambda origin: over_slots(lambda slot: close_rows(origin, slot)))
+    over_rows(lambda other: over_slots(lambda slot: relay_copy(other, slot).wait_send()))
+    over_rows(lambda other: col_remote(other).wait_send())
 
 
 def attention_kernel(
@@ -526,6 +576,7 @@
     head_count = chain_weight.shape[0]
     length = tile_rows * row_count
     own = tile_cols // row_count
+    span = col_count // row_count
     in_vmem = pl.BlockSpec(memory_space=pltpu.VMEM)
     dma = pltpu.SemaphoreType.DMA
     carried, normed, bias_rows = pl.pallas_call(
@@ -540,12 +591,17 @@
         scratch_shapes=[
             pltpu.VMEM((own, length, channels), jnp.bfloat16),
             pltpu.VMEM((own, length, channels), jnp.bfloat16),
-            dma((tile_rows // own,)),
+            pltpu.VMEM((row_count, span, own, tile_cols, channels), jnp.bfloat16),
+            dma((row_count, span)),
+            dma((row_count, span)),
+            dma((row_count, span)),
             dma((col_count,)),
             dma((row_count,)),
             dma((row_count,)),
-            dma((device_total,)),
-            dma((device_total,)),
+            dma((device_total // 2,)),
+            dma((device_total // 2,)),
+            dma((device_total // 2,)),
+            dma((device_total // 2,)),
         ],
         compiler_params=pltpu.CompilerParams(
             collective_id=0, has_side_effects=True, vmem_limit_bytes=VMEM_LIMIT
@@ -602,9 +658,9 @@
 
 def per_device(pair_state, *others):
     tile_cols = pair_state.shape[1]
-    row_count = lax.axis_size("row")
+    row_count, col_count = lax.axis_size("row"), lax.axis_size("col")
     own = tile_cols // row_count
-    if own % 8 == 0:
+    if own % 8 == 0 and col_count % 2 == 0 and col_count % row_count == 0:
         return owned_columns(pair_state, *others)
     return tile_layout(pair_state, *others)
 

time: 143 us -> 115 us (0.80)
  Pallas kernels: 133 us -> 106 us
    pallas_call x1, Pallas kernels: 82.2 us -> 57.9 us  [owned_columns(): pl.pallas_call(functools.partial(transition_kernel, row_count, col_count)...]
    pallas_call x1, Pallas kernels: 51.2 us -> 47.8 us  [owned_columns(): pl.pallas_call(functools.partial(attention_kernel, row_count, col_count),...]
where the time goes in v2:
time: 115 us
  Pallas kernels  106 us (92%)
  local copies, waits for them, and re-layouts  4.81 us (4%)
  other arithmetic  4.37 us (4%)
    pallas_call x1, Pallas kernels, owned_columns(): pl.pallas_call(functools.partial(transition_kernel, row_count, col_count)...  57.9 us
    pallas_call x1, Pallas kernels, owned_columns(): pl.pallas_call(functools.partial(attention_kernel, row_count, col_count),...  47.8 us
    sub x1, other arithmetic, owned_columns(): jnp.transpose(bias_rows, (1, 0, 2)).astype(jnp.float32)  2.84 us
    unnamed x3, local copies, waits for them, and re-layouts  2.54 us

profile of v2, /device:TPU:0, one launch (start us, length us, event | category | flops | bytes accessed | tf_op | source)
XLA Modules:
  0.0 114.9 jit_solution(10050251541401398069)
XLA Ops:
  0.0 0.7 convert_multiply_fusion
  0.7 0.9 compare_convert_fusion
  1.5 2.5 %copy.23 = bf16[128,16,256]{2,0,1:T(8,128)(2,1)} copy(bf16[128,16,256]{2,1,0:T(8,128)(2,1)} %tile_ref.1) | data formatting | bytes 2097152 | tf_op args[0]
  4.1 0.0 copy-start
  4.1 57.9 %transition.1 = (f32[8,256,256]{2,1,0:T(8,128)}, bf16[8,256,256]{2,1,0:T(8,128)(2,1)}, bf16[256,8,256]{2,1,0:T(8,128)(2,1)}) custom-call(bf16[128,16,256]{2,1,0:T(8,128)(2,1)} %tile_ref.1, bf16[16,128,256]{2,1,0:T(8,128)(2,1)} %bitcast.15, f32[1,256]{1,0:T(1,128)} %bitcast.17, bf16[256,1024]{1,0:T(8,128)(2,1)} %hidden_weight_ref.1, ...), custom_call_target="tpu_custom_call" | custom-call | tf_op jit(solution)/shard_map/transition/pallas_call | solution.py:582
  62.0 0.0 copy-done
  62.0 2.8 %fusion.bias_ref = f32[8,256,256]{2,1,0:T(8,128)} fusion(bf16[256,8,256]{2,1,0:T(8,128)(2,1)} %get-tuple-element.10, f32[256]{0:T(256)S(1)} %convert_multiply_fusion, f32[256,256]{1,0:T(8,128)S(1)} %compare_convert_fusion, f32[8]{0:T(128)S(1)} %copy-done), kind=kLoop, calls=%fused_computation.1 | loop fusion | flops 2097152 | bytes 3408928 | tf_op jit(solution)/shard_map/sub | solution.py:622
  64.8 47.8 %attention.1 = bf16[2,128,8,256]{3,2,1,0:T(8,128)(2,1)} custom-call(f32[8,256,256]{2,1,0:T(8,128)} %get-tuple-element.8.carried_ref, bf16[8,256,256]{2,1,0:T(8,128)(2,1)} %get-tuple-element.9.normed_ref, f32[8,256,256]{2,1,0:T(8,128)} %fusion.bias_ref, bf16[256,256]{1,0:T(8,128)(2,1)} %query_weight_ref.1, bf16[256,256]{1,0:T(8,128)(2,1)} %key_weight_ref.1, ...), custom_call_target="tpu_custom_call" | custom-call | tf_op jit(solution)/shard_map/attention/pallas_call | solution.py:626
  112.6 2.3 %copy_bitcast_fusion = bf16[128,16,256]{2,1,0:T(8,128)(2,1)} fusion(bf16[2,128,8,256]{3,2,1,0:T(8,128)(2,1)} %attention.1), kind=kLoop, calls=%fused_computation.2 | loop fusion | bytes 2097152 | tf_op jit(solution)/shard_map/reshape | solution.py:656
Async XLA Ops:
  4.1 57.9 %copy-start = (f32[8]{0:T(128)S(1)}, f32[8]{0:T(128)}, u32[]{:S(2)}) copy-start(f32[8]{0:T(128)} %param.26) | copy-start | bytes 100

commit v3 on v2

--- a/solution.py
+++ b/solution.py
@@ -10,6 +10,7 @@
 
 MESH = pl.DeviceIdType.MESH
 VMEM_LIMIT = 60 * 1024 * 1024
+LOG2_E = math.log2(math.e)
 
 mask_penalty = 1000000000.0
 norm_epsilon = 1e-05
@@ -423,10 +424,10 @@
     carried_ref,
     normed_ref,
     bias_ref,
-    query_weight_ref,
+    query_turned_ref,
     key_weight_ref,
-    value_weight_ref,
-    gate_weight_ref,
+    value_turned_ref,
+    gate_turned_ref,
     output_weight_ref,
     out_ref,
     total,
@@ -441,117 +442,138 @@
 ):
     own, length, channels = normed_ref.shape
     head_count = bias_ref.shape[0]
-    head_dim = query_weight_ref.shape[1] // head_count
-    score_scale = 1.0 / math.sqrt(head_dim)
-    tile_rows = length // row_count
+    inner_total = key_weight_ref.shape[1]
+    head_dim = inner_total // head_count
+    score_scale = LOG2_E / math.sqrt(head_dim)
     device_total = row_count * col_count
     row_id, col_id = lax.axis_index("row"), lax.axis_index("col")
     me = col_id * row_count + row_id
     greet_all(row_count, col_count)
 
-    def update_remote(position, peer):
-        return pltpu.make_async_remote_copy(
-            src_ref=update_buf.at[position, peer],
-            dst_ref=recv_buf.at[me * own + position],
-            send_sem=update_send.at[peer],
-            recv_sem=update_recv.at[me],
-            device_id=(lax.rem(peer, row_count), peer // row_count),
-            device_id_type=MESH,
-        )
-
-    head_of_lane = lax.broadcasted_iota(jnp.int32, (1, channels), 1) // head_dim
+    def over_peers(body):
+        def one(step, carry):
+            body(lax.rem(me + step, device_total))
+            return carry
+
+        lax.fori_loop(1, device_total, one, 0)
+
+    def over_rows(body):
+        def one(step, carry):
+            body(lax.rem(row_id + step, row_count))
+            return carry
+
+        lax.fori_loop(1, row_count, one, 0)
+
+    band = min(inner_total, max(128, head_dim))
+    heads_in_band = band // head_dim
+    head_of_lane = lax.broadcasted_iota(jnp.int32, (1, band), 1) // head_dim
 
     def one_row(position, carry):
         normed = normed_ref[position]
+        normed_turned = normed.T
 
         def project(weight_ref):
-            return jnp.dot(normed, weight_ref[...], preferred_element_type=jnp.float32)
-
-        queries = project(query_weight_ref).astype(jnp.bfloat16)
-        keys_turned = project(key_weight_ref).astype(jnp.bfloat16).T
-        values = project(value_weight_ref).astype(jnp.bfloat16)
-        gates = jax.nn.sigmoid(project(gate_weight_ref))
-        mixture = jnp.zeros((length, channels), jnp.float32)
+            return jnp.dot(weight_ref[...], normed_turned, preferred_element_type=jnp.float32)
+
+        keys = jnp.dot(
+            normed, key_weight_ref[...], preferred_element_type=jnp.float32
+        ).astype(jnp.bfloat16)
+        queries = project(query_turned_ref).astype(jnp.bfloat16)
+        values = project(value_turned_ref).astype(jnp.bfloat16)
+        gates = jax.nn.sigmoid(project(gate_turned_ref))
+        mixed = []
         for head in range(head_count):
-            chosen = (head_of_lane == head).astype(jnp.bfloat16)
+            first = head // heads_in_band * band
+            chosen = (head_of_lane == head % heads_in_band).astype(jnp.bfloat16)
+            rows = slice(head * head_dim, (head + 1) * head_dim)
             scores = (
-                jnp.dot(queries * chosen, keys_turned, preferred_element_type=jnp.float32)
+                jnp.dot(
+                    keys[:, first : first + band] * chosen,
+                    queries[first : first + band],
+                    preferred_element_type=jnp.float32,
+                )
                 * score_scale
                 + bias_ref[head]
             )
-            row_max = jnp.max(scores, axis=-1, keepdims=True)
-            exponent = jnp.exp(scores - row_max)
+            exponent = jnp.exp2(scores - jnp.max(scores, axis=0, keepdims=True))
             attn_weights = (
-                exponent * (1.0 / jnp.sum(exponent, axis=-1, keepdims=True))
+                exponent * (1.0 / jnp.sum(exponent, axis=0, keepdims=True))
             ).astype(jnp.bfloat16)
-            mixture = mixture + jnp.dot(
-                attn_weights, values * chosen, preferred_element_type=jnp.float32
-            )
-        gated = (gates * mixture).astype(jnp.bfloat16)
+            mixture = jnp.dot(values[rows], attn_weights, preferred_element_type=jnp.float32)
+            mixed.append((gates[rows] * mixture).astype(jnp.bfloat16))
+        gated = jnp.concatenate(mixed, axis=0).T
         update = jnp.dot(gated, output_weight_ref[...], preferred_element_type=jnp.float32)
         update = update.reshape(device_total, own, channels).astype(jnp.bfloat16)
         update_buf[position] = update
-        recv_buf[me * own + position] = update_buf[position, me]
+        recv_buf[me, position] = update_buf[position, me]
         total[position] = 2.0 * carried_ref[position] + update.astype(jnp.float32).reshape(
             length, channels
         )
-
-        def send(step, inner):
-            update_remote(position, lax.rem(me + step, device_total)).start()
-            return inner
-
-        lax.fori_loop(1, device_total, send, 0)
+        over_peers(
+            lambda peer: pltpu.make_async_remote_copy(
+                src_ref=update_buf.at[position, peer],
+                dst_ref=recv_buf.at[me, position],
+                send_sem=update_send.at[peer],
+                recv_sem=update_recv.at[position, me],
+                device_id=(lax.rem(peer, row_count), peer // row_count),
+                device_id_type=MESH,
+            ).start()
+        )
         return carry
 
     lax.fori_loop(0, own, one_row, 0)
     for position in range(own):
-        turned[:, position, :] = total[position]
-
-    def wait_update(step, carry):
-        peer = lax.rem(me + step, device_total)
-        landed = recv_buf.at[pl.ds(peer * own, own)]
-        pltpu.make_async_copy(landed, landed, update_recv.at[peer]).wait()
-        pltpu.make_async_copy(landed, landed, update_send.at[peer]).wait()
-        return carry
-
-    lax.fori_loop(1, device_total, wait_update, 0)
-
-    def sum_remote(other):
+        turned[:, :, position, :] = total[position].reshape(device_total, own, channels)
+
+    def summed(other, position):
+        devices = pl.ds(other * col_count, col_count)
+        return (
+            turned[devices, position] + recv_buf[devices, position].astype(jnp.float32)
+        ).astype(jnp.bfloat16)
+
+    def sum_remote(other, position):
         return pltpu.make_async_remote_copy(
-            src_ref=sum_buf.at[other],
-            dst_ref=out_ref.at[row_id],
-            send_sem=sum_send.at[other],
-            recv_sem=sum_recv.at[row_id],
+            src_ref=sum_buf.at[other, :, position],
+            dst_ref=out_ref.at[row_id, :, position],
+            send_sem=sum_send.at[other, position],
+            recv_sem=sum_recv.at[row_id, position],
             device_id=(other, col_id),
             device_id_type=MESH,
         )
 
-    def sum_rows(other, target_ref):
-        def one_block(block, carry):
-            rows = pl.ds(other * tile_rows + block * own, own)
-            summed = turned[rows] + recv_buf[rows].astype(jnp.float32)
-            target_ref[other, pl.ds(block * own, own)] = summed.astype(jnp.bfloat16)
-            return carry
-
-        lax.fori_loop(0, tile_rows // own, one_block, 0)
-
-    def send_sum(step, carry):
-        other = lax.rem(row_id + step, row_count)
-        sum_rows(other, sum_buf)
-        sum_remote(other).start()
+    def finish_position(position, carry):
+        def arrived(peer):
+            landed = recv_buf.at[peer, position]
+            pltpu.make_async_copy(landed, landed, update_recv.at[position, peer]).wait()
+
+        over_peers(arrived)
+
+        def pass_sum(other):
+            sum_buf[other, :, position] = summed(other, position)
+            sum_remote(other, position).start()
+
+        over_rows(pass_sum)
+        out_ref[row_id, :, position] = summed(row_id, position)
         return carry
 
-    lax.fori_loop(1, row_count, send_sum, 0)
-    sum_rows(row_id, out_ref)
-
-    def wait_sum(step, carry):
-        other = lax.rem(row_id + step, row_count)
-        landed = out_ref.at[other]
-        pltpu.make_async_copy(landed, landed, sum_recv.at[other]).wait()
-        sum_remote(other).wait_send()
+    lax.fori_loop(0, own, finish_position, 0)
+
+    def close_peer(peer):
+        sent = recv_buf.at[peer]
+        pltpu.make_async_copy(sent, sent, update_send.at[peer]).wait()
+
+    over_peers(close_peer)
+
+    def close_position(position, carry):
+        def close_row(other):
+            landed = out_ref.at[other, :, position]
+            pltpu.make_async_copy(landed, landed, sum_recv.at[other, position]).wait()
+            sum_remote(other, position).wait_send()
+
+        over_rows(close_row)
         return carry
 
-    lax.fori_loop(1, row_count, wait_sum, 0)
+    lax.fori_loop(0, own, close_position, 0)
 
 
 def owned_columns(
@@ -621,23 +643,23 @@
     bias_full = (
         jnp.transpose(bias_rows, (1, 0, 2)).astype(jnp.float32)
         + chain_weight[:, None, None] * same_chain[None]
-        - penalty[None, None, :]
-    )
+        - penalty[None, :, None]
+    ) * LOG2_E
     pieces = pl.pallas_call(
         functools.partial(attention_kernel, row_count, col_count),
-        out_shape=jax.ShapeDtypeStruct((row_count, tile_rows, own, channels), jnp.bfloat16),
+        out_shape=jax.ShapeDtypeStruct((row_count, col_count, own, own, channels), jnp.bfloat16),
         in_specs=[in_vmem] * 8,
         out_specs=in_vmem,
         scratch_shapes=[
             pltpu.VMEM((own, length, channels), jnp.float32),
             pltpu.VMEM((own, device_total, own, channels), jnp.bfloat16),
-            pltpu.VMEM((length, own, channels), jnp.bfloat16),
-            pltpu.VMEM((length, own, channels), jnp.float32),
-            pltpu.VMEM((row_count, tile_rows, own, channels), jnp.bfloat16),
+            pltpu.VMEM((device_total, own, own, channels), jnp.bfloat16),
+            pltpu.VMEM((device_total, own, own, channels), jnp.float32),
+            pltpu.VMEM((row_count, col_count, own, own, channels), jnp.bfloat16),
             dma((device_total,)),
-            dma((device_total,)),
-            dma((row_count,)),
-            dma((row_count,)),
+            dma((own, device_total)),
+            dma((row_count, own)),
+            dma((row_count, own)),
         ],
         compiler_params=pltpu.CompilerParams(
             collective_id=1, has_side_effects=True, vmem_limit_bytes=VMEM_LIMIT
@@ -647,12 +669,13 @@
         carried,
         normed,
         bias_full,
-        query_weight,
+        query_weight.T,
         key_weight,
-        value_weight,
-        gate_weight,
+        value_weight.T,
+        gate_weight.T,
         output_weight,
     )
+    pieces = pieces.reshape(row_count, tile_rows, own, channels)
     return jnp.transpose(pieces, (1, 0, 2, 3)).reshape(tile_rows, tile_cols, channels)
 
 

time: 115 us -> 123 us (1.070)
  Pallas kernels: 106 us -> 113 us
  local copies, waits for them, and re-layouts: 4.81 us -> 7.11 us
  other arithmetic: 4.37 us -> 3.05 us
    pallas_call x1, Pallas kernels: 47.8 us -> 54.9 us  [owned_columns(): pl.pallas_call(functools.partial(attention_kernel, row_count, col_count),...]
    mul x0 -> x1, other arithmetic: none -> 2.94 us  [owned_columns(): (jnp.transpose(bias_rows, (1, 0, 2)).astype(jnp.float32) + chain_weight[:...]
    sub x1 -> x0, other arithmetic: 2.84 us -> none  [owned_columns(): jnp.transpose(bias_rows, (1, 0, 2)).astype(jnp.float32)]
    unnamed x3 -> x16, local copies, waits for them, and re-layouts: 2.54 us -> 4.83 us
    reshape x1 -> x0, local copies, waits for them, and re-layouts: 2.28 us -> none  [owned_columns(): jnp.transpose(pieces, (1, 0, 2, 3)).reshape(tile_rows, tile_cols, channels)]
    transpose x0 -> x1, local copies, waits for them, and re-layouts: none -> 2.28 us  [owned_columns(): jnp.transpose(pieces, (1, 0, 2, 3)).reshape(tile_rows, tile_cols, channels)]
where the time goes in v3:
time: 123 us
  Pallas kernels  113 us (92%)
  local copies, waits for them, and re-layouts  7.11 us (6%)
  other arithmetic  3.05 us (2%)
    pallas_call x1, Pallas kernels, owned_columns(): pl.pallas_call(functools.partial(transition_kernel, row_count, col_count)...  57.9 us
    pallas_call x1, Pallas kernels, owned_columns(): pl.pallas_call(functools.partial(attention_kernel, row_count, col_count),...  54.9 us
    unnamed x16, local copies, waits for them, and re-layouts  4.83 us
    mul x1, other arithmetic, owned_columns(): (jnp.transpose(bias_rows, (1, 0, 2)).astype(jnp.float32) + chain_weight[:...  2.94 us

profile of v3, /device:TPU:0, one launch (start us, length us, event | category | flops | bytes accessed | tf_op | source)
XLA Modules:
  0.0 123.0 jit_solution(4504741484769252582)
XLA Ops:
  0.0 2.5 %copy.25 = bf16[128,16,256]{2,0,1:T(8,128)(2,1)} copy(bf16[128,16,256]{2,1,0:T(8,128)(2,1)} %tile_ref.1) | data formatting | bytes 2097152 | tf_op args[0]
  2.5 0.0 copy-start.3
  2.5 0.0 copy-start.4
  2.5 0.0 copy-start.5
  2.5 57.9 %transition.1 = (f32[8,256,256]{2,1,0:T(8,128)}, bf16[8,256,256]{2,1,0:T(8,128)(2,1)}, bf16[256,8,256]{2,1,0:T(8,128)(2,1)}) custom-call(bf16[128,16,256]{2,1,0:T(8,128)(2,1)} %tile_ref.1, bf16[16,128,256]{2,1,0:T(8,128)(2,1)} %bitcast.21, f32[1,256]{1,0:T(1,128)} %bitcast.27, bf16[256,1024]{1,0:T(8,128)(2,1)} %hidden_weight_ref.1, ...), custom_call_target="tpu_custom_call" | custom-call | tf_op jit(solution)/shard_map/transition/pallas_call | solution.py:604
  60.5 0.0 copy-start
  60.5 0.0 copy-start.1
  60.5 0.0 copy-done.3
  60.5 0.0 copy-start.2
  60.5 0.1 compare_convert_fusion
  60.6 0.0 copy-done.4
  60.6 0.0 copy-done.5
  60.7 2.9 %fusion.1.bias_ref = f32[8,256,256]{2,1,0:T(8,128)} fusion(bf16[256,8,256]{2,1,0:T(8,128)(2,1)} %get-tuple-element.10, f32[256]{0:T(256)S(1)} %convert_multiply_fusion, f32[256,256]{1,0:T(8,128)S(1)} %compare_convert_fusion, f32[8]{0:T(128)S(1)} %copy-done.5), kind=kLoop, calls=%fused_computation.2 | loop fusion | flops 2621440 | bytes 3408928 | tf_op jit(solution)/shard_map/mul | solution.py:643
  63.6 0.0 copy-done
  63.6 0.8 copy.17
  64.4 0.0 copy-done.1
  64.4 0.8 copy.18
  65.1 0.0 copy-done.2
  65.1 0.7 copy.19
  65.9 54.9 %attention.1 = bf16[2,16,8,8,256]{4,3,2,1,0:T(8,128)(2,1)} custom-call(f32[8,256,256]{2,1,0:T(8,128)} %get-tuple-element.8.carried_ref, bf16[8,256,256]{2,1,0:T(8,128)(2,1)} %get-tuple-element.9.normed_ref, f32[8,256,256]{2,1,0:T(8,128)} %fusion.1.bias_ref, bf16[256,256]{1,0:T(8,128)(2,1)} %bitcast.23, bf16[256,256]{1,0:T(8,128)(2,1)} %key_weight_ref.1, ...), custom_call_target="tpu_custom_call" | custom-call | tf_op jit(solution)/shard_map/attention/pallas_call | solution.py:648
  120.8 2.3 %copy.24 = bf16[128,2,8,256]{3,2,1,0:T(8,128)(2,1)} copy(bf16[128,2,8,256]{3,2,0,1:T(8,128)(2,1)} %bitcast.22) | data formatting | bytes 2097152 | tf_op jit(solution)/shard_map/transpose | solution.py:679
  (1 shorter events, 0.0 us)
Async XLA Ops:
  2.5 58.0 %copy-start.3 = (s32[256]{0:T(256)S(1)}, s32[256]{0:T(256)}, u32[]{:S(2)}) copy-start(s32[256]{0:T(256)} %param.16) | copy-start | bytes 3076
  2.5 58.1 %copy-start.4 = (s32[256]{0:T(256)S(1)}, s32[256]{0:T(256)}, u32[]{:S(2)}) copy-start(s32[256]{0:T(256)} %param.15) | copy-start | bytes 3076
  2.5 58.1 %copy-start.5 = (f32[8]{0:T(128)S(1)}, f32[8]{0:T(128)}, u32[]{:S(2)}) copy-start(f32[8]{0:T(128)} %param.26) | copy-start | bytes 100
  60.5 3.1 %copy-start = (bf16[256,256]{1,0:T(8,128)(2,1)S(1)}, bf16[256,256]{1,0:T(8,128)(2,1)}, u32[]{:S(2)}) copy-start(bf16[256,256]{1,0:T(8,128)(2,1)} %param.21) | copy-start | bytes 393220
  60.5 3.9 %copy-start.1 = (bf16[256,256]{1,0:T(8,128)(2,1)S(1)}, bf16[256,256]{1,0:T(8,128)(2,1)}, u32[]{:S(2)}) copy-start(bf16[256,256]{1,0:T(8,128)(2,1)} %param.23) | copy-start | bytes 393220
  60.5 4.6 %copy-start.2 = (bf16[256,256]{1,0:T(8,128)(2,1)S(1)}, bf16[256,256]{1,0:T(8,128)(2,1)}, u32[]{:S(2)}) copy-start(bf16[256,256]{1,0:T(8,128)(2,1)} %param.24) | copy-start | bytes 393220

commit v4 on v3

--- a/solution.py
+++ b/solution.py
@@ -435,6 +435,8 @@
     recv_buf,
     turned,
     sum_buf,
+    score_buf,
+    weight_buf,
     update_send,
     update_recv,
     sum_send,
@@ -464,6 +466,7 @@
 
         lax.fori_loop(1, row_count, one, 0)
 
+    strip = min(128, length)
     band = min(inner_total, max(128, head_dim))
     heads_in_band = band // head_dim
     head_of_lane = lax.broadcasted_iota(jnp.int32, (1, band), 1) // head_dim
@@ -481,12 +484,10 @@
         queries = project(query_turned_ref).astype(jnp.bfloat16)
         values = project(value_turned_ref).astype(jnp.bfloat16)
         gates = jax.nn.sigmoid(project(gate_turned_ref))
-        mixed = []
         for head in range(head_count):
             first = head // heads_in_band * band
             chosen = (head_of_lane == head % heads_in_band).astype(jnp.bfloat16)
-            rows = slice(head * head_dim, (head + 1) * head_dim)
-            scores = (
+            score_buf[head] = (
                 jnp.dot(
                     keys[:, first : first + band] * chosen,
                     queries[first : first + band],
@@ -495,11 +496,17 @@
                 * score_scale
                 + bias_ref[head]
             )
-            exponent = jnp.exp2(scores - jnp.max(scores, axis=0, keepdims=True))
-            attn_weights = (
-                exponent * (1.0 / jnp.sum(exponent, axis=0, keepdims=True))
-            ).astype(jnp.bfloat16)
-            mixture = jnp.dot(values[rows], attn_weights, preferred_element_type=jnp.float32)
+        mixed = []
+        for head in range(head_count):
+            rows = slice(head * head_dim, (head + 1) * head_dim)
+            for start in range(0, length, strip):
+                places = slice(start, start + strip)
+                scores = score_buf[head, :, places]
+                exponent = jnp.exp2(scores - jnp.max(scores, axis=0, keepdims=True))
+                weight_buf[head, :, places] = (
+                    exponent * (1.0 / jnp.sum(exponent, axis=0, keepdims=True))
+                ).astype(jnp.bfloat16)
+            mixture = jnp.dot(values[rows], weight_buf[head], preferred_element_type=jnp.float32)
             mixed.append((gates[rows] * mixture).astype(jnp.bfloat16))
         gated = jnp.concatenate(mixed, axis=0).T
         update = jnp.dot(gated, output_weight_ref[...], preferred_element_type=jnp.float32)
@@ -656,6 +663,8 @@
             pltpu.VMEM((device_total, own, own, channels), jnp.bfloat16),
             pltpu.VMEM((device_total, own, own, channels), jnp.float32),
             pltpu.VMEM((row_count, col_count, own, own, channels), jnp.bfloat16),
+            pltpu.VMEM((head_count, length, length), jnp.float32),
+            pltpu.VMEM((head_count, length, length), jnp.bfloat16),
             dma((device_total,)),
             dma((own, device_total)),
             dma((row_count, own)),

time: 123 us -> 112 us (0.911)
  Pallas kernels: 113 us -> 102 us
    pallas_call x1, Pallas kernels: 54.9 us -> 44 us  [owned_columns(): pl.pallas_call(functools.partial(attention_kernel, row_count, col_count),...]
where the time goes in v4:
time: 112 us
  Pallas kernels  102 us (91%)
  local copies, waits for them, and re-layouts  7.11 us (6%)
  other arithmetic  3.05 us (3%)
    pallas_call x1, Pallas kernels, owned_columns(): pl.pallas_call(functools.partial(transition_kernel, row_count, col_count)...  57.9 us
    pallas_call x1, Pallas kernels, owned_columns(): pl.pallas_call(functools.partial(attention_kernel, row_count, col_count),...  44 us
    unnamed x16, local copies, waits for them, and re-layouts  4.83 us
    mul x1, other arithmetic, owned_columns(): (jnp.transpose(bias_rows, (1, 0, 2)).astype(jnp.float32) + chain_weight[:...  2.94 us
    transpose x1, local copies, waits for them, and re-layouts, owned_columns(): jnp.transpose(pieces, (1, 0, 2, 3)).reshape(tile_rows, tile_cols, channels)  2.28 us

profile of v4, /device:TPU:0, one launch (start us, length us, event | category | flops | bytes accessed | tf_op | source)
XLA Modules:
  0.0 112.2 jit_solution(16920347862803630450)
XLA Ops:
  0.0 2.5 %copy.25 = bf16[128,16,256]{2,0,1:T(8,128)(2,1)} copy(bf16[128,16,256]{2,1,0:T(8,128)(2,1)} %tile_ref.1) | data formatting | bytes 2097152 | tf_op args[0]
  2.5 0.0 copy-start.3
  2.5 0.0 copy-start.4
  2.5 0.0 copy-start.5
  2.5 57.9 %transition.1 = (f32[8,256,256]{2,1,0:T(8,128)}, bf16[8,256,256]{2,1,0:T(8,128)(2,1)}, bf16[256,8,256]{2,1,0:T(8,128)(2,1)}) custom-call(bf16[128,16,256]{2,1,0:T(8,128)(2,1)} %tile_ref.1, bf16[16,128,256]{2,1,0:T(8,128)(2,1)} %bitcast.21, f32[1,256]{1,0:T(1,128)} %bitcast.27, bf16[256,1024]{1,0:T(8,128)(2,1)} %hidden_weight_ref.1, ...), custom_call_target="tpu_custom_call" | custom-call | tf_op jit(solution)/shard_map/transition/pallas_call | solution.py:611
  60.5 0.0 copy-start
  60.5 0.0 copy-start.1
  60.5 0.0 copy-done.3
  60.5 0.0 copy-start.2
  60.5 0.1 compare_convert_fusion
  60.6 0.0 copy-done.4
  60.6 0.0 copy-done.5
  60.7 2.9 %fusion.1.bias_ref = f32[8,256,256]{2,1,0:T(8,128)} fusion(bf16[256,8,256]{2,1,0:T(8,128)(2,1)} %get-tuple-element.10, f32[256]{0:T(256)S(1)} %convert_multiply_fusion, f32[256,256]{1,0:T(8,128)S(1)} %compare_convert_fusion, f32[8]{0:T(128)S(1)} %copy-done.5), kind=kLoop, calls=%fused_computation.2 | loop fusion | flops 2621440 | bytes 3408928 | tf_op jit(solution)/shard_map/mul | solution.py:650
  63.6 0.0 copy-done
  63.6 0.8 copy.17
  64.4 0.0 copy-done.1
  64.4 0.8 copy.18
  65.1 0.0 copy-done.2
  65.1 0.7 copy.19
  65.9 44.0 %attention.1 = bf16[2,16,8,8,256]{4,3,2,1,0:T(8,128)(2,1)} custom-call(f32[8,256,256]{2,1,0:T(8,128)} %get-tuple-element.8.carried_ref, bf16[8,256,256]{2,1,0:T(8,128)(2,1)} %get-tuple-element.9.normed_ref, f32[8,256,256]{2,1,0:T(8,128)} %fusion.1.bias_ref, bf16[256,256]{1,0:T(8,128)(2,1)} %bitcast.23, bf16[256,256]{1,0:T(8,128)(2,1)} %key_weight_ref.1, ...), custom_call_target="tpu_custom_call" | custom-call | tf_op jit(solution)/shard_map/attention/pallas_call | solution.py:655
  109.9 2.3 %copy.24 = bf16[128,2,8,256]{3,2,1,0:T(8,128)(2,1)} copy(bf16[128,2,8,256]{3,2,0,1:T(8,128)(2,1)} %bitcast.22) | data formatting | bytes 2097152 | tf_op jit(solution)/shard_map/transpose | solution.py:688
  (1 shorter events, 0.0 us)
Async XLA Ops:
  2.5 58.0 %copy-start.3 = (s32[256]{0:T(256)S(1)}, s32[256]{0:T(256)}, u32[]{:S(2)}) copy-start(s32[256]{0:T(256)} %param.16) | copy-start | bytes 3076
  2.5 58.1 %copy-start.4 = (s32[256]{0:T(256)S(1)}, s32[256]{0:T(256)}, u32[]{:S(2)}) copy-start(s32[256]{0:T(256)} %param.15) | copy-start | bytes 3076
  2.5 58.1 %copy-start.5 = (f32[8]{0:T(128)S(1)}, f32[8]{0:T(128)}, u32[]{:S(2)}) copy-start(f32[8]{0:T(128)} %param.26) | copy-start | bytes 100
  60.5 3.1 %copy-start = (bf16[256,256]{1,0:T(8,128)(2,1)S(1)}, bf16[256,256]{1,0:T(8,128)(2,1)}, u32[]{:S(2)}) copy-start(bf16[256,256]{1,0:T(8,128)(2,1)} %param.21) | copy-start | bytes 393220
  60.5 3.9 %copy-start.1 = (bf16[256,256]{1,0:T(8,128)(2,1)S(1)}, bf16[256,256]{1,0:T(8,128)(2,1)}, u32[]{:S(2)}) copy-start(bf16[256,256]{1,0:T(8,128)(2,1)} %param.23) | copy-start | bytes 393220
  60.5 4.6 %copy-start.2 = (bf16[256,256]{1,0:T(8,128)(2,1)S(1)}, bf16[256,256]{1,0:T(8,128)(2,1)}, u32[]{:S(2)}) copy-start(bf16[256,256]{1,0:T(8,128)(2,1)} %param.24) | copy-start | bytes 393220

commit v5 on v4

--- a/solution.py
+++ b/solution.py
@@ -424,10 +424,10 @@
     carried_ref,
     normed_ref,
     bias_ref,
-    query_turned_ref,
+    query_weight_ref,
     key_weight_ref,
-    value_turned_ref,
-    gate_turned_ref,
+    value_weight_ref,
+    gate_weight_ref,
     output_weight_ref,
     out_ref,
     total,
@@ -437,6 +437,9 @@
     sum_buf,
     score_buf,
     weight_buf,
+    query_turned,
+    value_turned,
+    gate_turned,
     update_send,
     update_recv,
     sum_send,
@@ -450,6 +453,9 @@
     device_total = row_count * col_count
     row_id, col_id = lax.axis_index("row"), lax.axis_index("col")
     me = col_id * row_count + row_id
+    query_turned[...] = query_weight_ref[...].T
+    value_turned[...] = value_weight_ref[...].T
+    gate_turned[...] = gate_weight_ref[...].T
     greet_all(row_count, col_count)
 
     def over_peers(body):
@@ -481,10 +487,10 @@
         keys = jnp.dot(
             normed, key_weight_ref[...], preferred_element_type=jnp.float32
         ).astype(jnp.bfloat16)
-        queries = project(query_turned_ref).astype(jnp.bfloat16)
-        values = project(value_turned_ref).astype(jnp.bfloat16)
-        gates = jax.nn.sigmoid(project(gate_turned_ref))
-        for head in range(head_count):
+        queries = project(query_turned).astype(jnp.bfloat16)
+        values = project(value_turned).astype(jnp.bfloat16)
+        gates = jax.nn.sigmoid(project(gate_turned))
+        def score(head):
             first = head // heads_in_band * band
             chosen = (head_of_lane == head % heads_in_band).astype(jnp.bfloat16)
             score_buf[head] = (
@@ -496,8 +502,13 @@
                 * score_scale
                 + bias_ref[head]
             )
+
         mixed = []
+        for head in range(4):
+            score(head)
         for head in range(head_count):
+            if head + 4 < head_count:
+                score(head + 4)
             rows = slice(head * head_dim, (head + 1) * head_dim)
             for start in range(0, length, strip):
                 places = slice(start, start + strip)
@@ -665,6 +676,9 @@
             pltpu.VMEM((row_count, col_count, own, own, channels), jnp.bfloat16),
             pltpu.VMEM((head_count, length, length), jnp.float32),
             pltpu.VMEM((head_count, length, length), jnp.bfloat16),
+            pltpu.VMEM(query_weight.shape[::-1], jnp.bfloat16),
+            pltpu.VMEM(value_weight.shape[::-1], jnp.bfloat16),
+            pltpu.VMEM(gate_weight.shape[::-1], jnp.bfloat16),
             dma((device_total,)),
             dma((own, device_total)),
             dma((row_count, own)),
@@ -678,10 +692,10 @@
         carried,
         normed,
         bias_full,
-        query_weight.T,
+        query_weight,
         key_weight,
-        value_weight.T,
-        gate_weight.T,
+        value_weight,
+        gate_weight,
         output_weight,
     )
     pieces = pieces.reshape(row_count, tile_rows, own, channels)

time: 112 us -> 112 us (level)
  local copies, waits for them, and re-layouts: 7.11 us -> 4.81 us
  other arithmetic: 3.05 us -> 4.43 us
    unnamed x16 -> x3, local copies, waits for them, and re-layouts: 4.83 us -> 2.54 us
where the time goes in v5:
time: 112 us; the launch traced here: 111 us
  Pallas kernels  102 us (91%)
  local copies, waits for them, and re-layouts  4.81 us (4%)
  other arithmetic  4.43 us (4%)
    pallas_call x1, Pallas kernels, owned_columns(): pl.pallas_call(functools.partial(transition_kernel, row_count, col_count)...  57.9 us
    pallas_call x1, Pallas kernels, owned_columns(): pl.pallas_call(functools.partial(attention_kernel, row_count, col_count),...  44.2 us
    mul x1, other arithmetic, owned_columns(): (jnp.transpose(bias_rows, (1, 0, 2)).astype(jnp.float32) + chain_weight[:...  2.9 us
    unnamed x3, local copies, waits for them, and re-layouts  2.54 us
    transpose x1, local copies, waits for them, and re-layouts, owned_columns(): jnp.transpose(pieces, (1, 0, 2, 3)).reshape(tile_rows, tile_cols, channels)  2.28 us

profile of v5, /device:TPU:0, one launch (start us, length us, event | category | flops | bytes accessed | tf_op | source)
XLA Modules:
  0.0 111.4 jit_solution(15758513563388534610)
XLA Ops:
  0.0 0.7 convert_multiply_fusion
  0.7 0.9 compare_convert_fusion
  1.5 2.5 %copy.22 = bf16[128,16,256]{2,0,1:T(8,128)(2,1)} copy(bf16[128,16,256]{2,1,0:T(8,128)(2,1)} %tile_ref.1) | data formatting | bytes 2097152 | tf_op args[0]
  4.1 0.0 copy-start
  4.1 57.9 %transition.1 = (f32[8,256,256]{2,1,0:T(8,128)}, bf16[8,256,256]{2,1,0:T(8,128)(2,1)}, bf16[256,8,256]{2,1,0:T(8,128)(2,1)}) custom-call(bf16[128,16,256]{2,1,0:T(8,128)(2,1)} %tile_ref.1, bf16[16,128,256]{2,1,0:T(8,128)(2,1)} %bitcast.18, f32[1,256]{1,0:T(1,128)} %bitcast.21, bf16[256,1024]{1,0:T(8,128)(2,1)} %hidden_weight_ref.1, ...), custom_call_target="tpu_custom_call" | custom-call | tf_op jit(solution)/shard_map/transition/pallas_call | solution.py:622
  62.0 0.0 copy-done
  62.0 2.9 %fusion.1.bias_ref = f32[8,256,256]{2,1,0:T(8,128)} fusion(bf16[256,8,256]{2,1,0:T(8,128)(2,1)} %get-tuple-element.10, f32[256]{0:T(256)S(1)} %convert_multiply_fusion, f32[256,256]{1,0:T(8,128)S(1)} %compare_convert_fusion, f32[8]{0:T(128)S(1)} %copy-done), kind=kLoop, calls=%fused_computation.2 | loop fusion | flops 2621440 | bytes 3408928 | tf_op jit(solution)/shard_map/mul | solution.py:661
  64.9 44.2 %attention.1 = bf16[2,16,8,8,256]{4,3,2,1,0:T(8,128)(2,1)} custom-call(f32[8,256,256]{2,1,0:T(8,128)} %get-tuple-element.8.carried_ref, bf16[8,256,256]{2,1,0:T(8,128)(2,1)} %get-tuple-element.9.normed_ref, f32[8,256,256]{2,1,0:T(8,128)} %fusion.1.bias_ref, bf16[256,256]{1,0:T(8,128)(2,1)} %query_weight_ref.1, bf16[256,256]{1,0:T(8,128)(2,1)} %key_weight_ref.1, ...), custom_call_target="tpu_custom_call" | custom-call | tf_op jit(solution)/shard_map/attention/pallas_call | solution.py:666
  109.1 2.3 %copy.21 = bf16[128,2,8,256]{3,2,1,0:T(8,128)(2,1)} copy(bf16[128,2,8,256]{3,2,0,1:T(8,128)(2,1)} %bitcast.19) | data formatting | bytes 2097152 | tf_op jit(solution)/shard_map/transpose | solution.py:702
Async XLA Ops:
  4.1 57.9 %copy-start = (f32[8]{0:T(128)S(1)}, f32[8]{0:T(128)}, u32[]{:S(2)}) copy-start(f32[8]{0:T(128)} %param.26) | copy-start | bytes 100

commit v6 on v5

--- a/solution.py
+++ b/solution.py
@@ -229,6 +229,7 @@
 ):
     tile_rows, tile_cols, channels = tile_ref.shape
     own = tile_cols // row_count
+    half = own // 2
     span = col_count // row_count
     chip_total = row_count * col_count // 2
     row_id, col_id = lax.axis_index("row"), lax.axis_index("col")
@@ -237,43 +238,44 @@
     chip = (col_id // 2) * row_count + row_id
     greet_all(row_count, col_count)
 
-    def relay_copy(other, slot):
+    def relay_copy(other, slot, part):
         return pltpu.make_async_remote_copy(
-            src_ref=tile_ref.at[pl.ds((slot * row_count + other) * own, own)],
-            dst_ref=relay_buf.at[row_id, slot],
-            send_sem=relay_send.at[other, slot],
-            recv_sem=relay_recv.at[row_id, slot],
+            src_ref=tile_ref.at[pl.ds((slot * row_count + other) * own + part * half, half)],
+            dst_ref=relay_buf.at[row_id, slot, part],
+            send_sem=relay_send.at[other, slot, part],
+            recv_sem=relay_recv.at[row_id, slot, part],
             device_id=(other, col_id),
             device_id_type=MESH,
         )
 
-    def start_rows(origin, slot, source):
+    def start_rows(origin, slot, part, source):
         target = origin * span + slot
-        landing = row_buf.at[:, pl.ds(pl.multiple_of(col_id * tile_cols, tile_cols), tile_cols), :]
+        columns = pl.ds(pl.multiple_of(col_id * tile_cols, tile_cols), tile_cols)
+        landing = row_buf.at[pl.ds(part * half, half), columns, :]
 
         @pl.when(target != col_id)
         def _():
             pltpu.make_async_remote_copy(
                 src_ref=source,
                 dst_ref=landing,
-                send_sem=row_send.at[origin, slot],
-                recv_sem=row_recv.at[col_id],
+                send_sem=row_send.at[origin, slot, part],
+                recv_sem=row_recv.at[col_id, part],
                 device_id=(row_id, target),
                 device_id_type=MESH,
             ).start()
 
         @pl.when(target == col_id)
         def _():
-            pltpu.make_async_copy(source, landing, row_recv.at[col_id]).start()
-
-    def col_remote(other):
+            pltpu.make_async_copy(source, landing, row_recv.at[col_id, part]).start()
+
+    def col_remote(other, part):
         return pltpu.make_async_remote_copy(
-            src_ref=turned_ref.at[pl.ds(other * own, own)],
+            src_ref=turned_ref.at[pl.ds(other * own + part * half, half)],
             dst_ref=col_buf.at[
-                :, pl.ds(pl.multiple_of(row_id * tile_rows, tile_rows), tile_rows), :
+                pl.ds(part * half, half), pl.ds(pl.multiple_of(row_id * tile_rows, tile_rows), tile_rows), :
             ],
-            send_sem=col_send.at[other],
-            recv_sem=col_recv.at[row_id],
+            send_sem=col_send.at[other, part],
+            recv_sem=col_recv.at[row_id, part],
             device_id=(other, col_id),
             device_id_type=MESH,
         )
@@ -292,40 +294,49 @@
 
         lax.fori_loop(0, span, one, 0)
 
-    over_rows(lambda other: over_slots(lambda slot: relay_copy(other, slot).start()))
-    over_slots(
-        lambda slot: start_rows(
-            row_id, slot, tile_ref.at[pl.ds((slot * row_count + row_id) * own, own)]
-        )
-    )
-    over_rows(lambda other: col_remote(other).start())
-    own_col = pltpu.make_async_copy(
-        turned_ref.at[pl.ds(row_id * own, own)],
-        col_buf.at[:, pl.ds(pl.multiple_of(row_id * tile_rows, tile_rows), tile_rows), :],
-        col_recv.at[row_id],
-    )
-    own_col.start()
-
-    def pass_on(origin, slot):
-        arrived = relay_buf.at[origin, slot]
-        pltpu.make_async_copy(arrived, arrived, relay_recv.at[origin, slot]).wait()
-        start_rows(origin, slot, arrived)
-
-    over_rows(lambda origin: over_slots(lambda slot: pass_on(origin, slot)))
-
-    def wait_row(other, carry):
-        landed = row_buf.at[:, pl.ds(pl.multiple_of(other * tile_cols, tile_cols), tile_cols), :]
-        pltpu.make_async_copy(landed, landed, row_recv.at[other]).wait()
-        return carry
-
-    lax.fori_loop(0, col_count, wait_row, 0)
-
-    def wait_col(other, carry):
-        landed = col_buf.at[:, pl.ds(pl.multiple_of(other * tile_rows, tile_rows), tile_rows), :]
-        pltpu.make_async_copy(landed, landed, col_recv.at[other]).wait()
-        return carry
-
-    lax.fori_loop(0, row_count, wait_col, 0)
+    own_columns = pl.ds(pl.multiple_of(row_id * tile_rows, tile_rows), tile_rows)
+
+    def own_col(part):
+        return pltpu.make_async_copy(
+            turned_ref.at[pl.ds(row_id * own + part * half, half)],
+            col_buf.at[pl.ds(part * half, half), own_columns, :],
+            col_recv.at[row_id, part],
+        )
+
+    def direct(slot, part):
+        first = (slot * row_count + row_id) * own + part * half
+        start_rows(row_id, slot, part, tile_ref.at[pl.ds(first, half)])
+
+    def pass_on(origin, slot, part):
+        arrived = relay_buf.at[origin, slot, part]
+        pltpu.make_async_copy(arrived, arrived, relay_recv.at[origin, slot, part]).wait()
+        start_rows(origin, slot, part, arrived)
+
+    for part in range(2):
+        over_rows(lambda other: over_slots(lambda slot: relay_copy(other, slot, part).start()))
+    for part in range(2):
+        over_slots(lambda slot: direct(slot, part))
+        over_rows(lambda other: col_remote(other, part).start())
+        own_col(part).start()
+    for part in range(2):
+        over_rows(lambda origin: over_slots(lambda slot: pass_on(origin, slot, part)))
+
+    def wait_part(part):
+        def wait_row(other, carry):
+            columns = pl.ds(pl.multiple_of(other * tile_cols, tile_cols), tile_cols)
+            landed = row_buf.at[pl.ds(part * half, half), columns, :]
+            pltpu.make_async_copy(landed, landed, row_recv.at[other, part]).wait()
+            return carry
+
+        lax.fori_loop(0, col_count, wait_row, 0)
+
+        def wait_col(other, carry):
+            columns = pl.ds(pl.multiple_of(other * tile_rows, tile_rows), tile_rows)
+            landed = col_buf.at[pl.ds(part * half, half), columns, :]
+            pltpu.make_async_copy(landed, landed, col_recv.at[other, part]).wait()
+            return carry
+
+        lax.fori_loop(0, row_count, wait_col, 0)
 
     def over_chips(body):
         def one(step, carry):
@@ -371,7 +382,12 @@
         )
         return carry
 
-    lax.fori_loop(0, own, one_row, 0)
+    def part_rows(part, carry):
+        wait_part(part)
+        lax.fori_loop(part * half, (part + 1) * half, one_row, 0)
+        return carry
+
+    lax.fori_loop(0, 2, part_rows, 0)
 
     def to_pair(other):
         return pltpu.make_async_remote_copy(
@@ -406,16 +422,17 @@
 
     over_chips(close_chip)
 
-    def close_rows(origin, slot):
+    def close_rows(origin, slot, part):
         @pl.when(origin * span + slot != col_id)
         def _():
-            sent = relay_buf.at[origin, slot]
-            pltpu.make_async_copy(sent, sent, row_send.at[origin, slot]).wait()
-
-    over_slots(lambda slot: close_rows(row_id, slot))
-    over_rows(lambda origin: over_slots(lambda slot: close_rows(origin, slot)))
-    over_rows(lambda other: over_slots(lambda slot: relay_copy(other, slot).wait_send()))
-    over_rows(lambda other: col_remote(other).wait_send())
+            sent = relay_buf.at[origin, slot, part]
+            pltpu.make_async_copy(sent, sent, row_send.at[origin, slot, part]).wait()
+
+    for part in range(2):
+        over_slots(lambda slot: close_rows(row_id, slot, part))
+        over_rows(lambda origin: over_slots(lambda slot: close_rows(origin, slot, part)))
+        over_rows(lambda other: over_slots(lambda slot: relay_copy(other, slot, part).wait_send()))
+        over_rows(lambda other: col_remote(other, part).wait_send())
 
 
 def attention_kernel(
@@ -631,13 +648,13 @@
         scratch_shapes=[
             pltpu.VMEM((own, length, channels), jnp.bfloat16),
             pltpu.VMEM((own, length, channels), jnp.bfloat16),
-            pltpu.VMEM((row_count, span, own, tile_cols, channels), jnp.bfloat16),
-            dma((row_count, span)),
-            dma((row_count, span)),
-            dma((row_count, span)),
-            dma((col_count,)),
-            dma((row_count,)),
-            dma((row_count,)),
+            pltpu.VMEM((row_count, span, 2, own // 2, tile_cols, channels), jnp.bfloat16),
+            dma((row_count, span, 2)),
+            dma((row_count, span, 2)),
+            dma((row_count, span, 2)),
+            dma((col_count, 2)),
+            dma((row_count, 2)),
+            dma((row_count, 2)),
             dma((device_total // 2,)),
             dma((device_total // 2,)),
             dma((device_total // 2,)),

time: 112 us -> 109 us (0.973)
  Pallas kernels: 102 us -> 99.7 us
    pallas_call x1, Pallas kernels: 57.9 us -> 55.5 us  [owned_columns(): pl.pallas_call(functools.partial(transition_kernel, row_count, col_count)...]
where the time goes in v6:
time: 109 us
  Pallas kernels  99.7 us (91%)
  local copies, waits for them, and re-layouts  4.81 us (4%)
  other arithmetic  4.43 us (4%)
    pallas_call x1, Pallas kernels, owned_columns(): pl.pallas_call(functools.partial(transition_kernel, row_count, col_count)...  55.5 us
    pallas_call x1, Pallas kernels, owned_columns(): pl.pallas_call(functools.partial(attention_kernel, row_count, col_count),...  44.2 us
    mul x1, other arithmetic, owned_columns(): (jnp.transpose(bias_rows, (1, 0, 2)).astype(jnp.float32) + chain_weight[:...  2.9 us
    unnamed x3, local copies, waits for them, and re-layouts  2.54 us
    transpose x1, local copies, waits for them, and re-layouts, owned_columns(): jnp.transpose(pieces, (1, 0, 2, 3)).reshape(tile_rows, tile_cols, channels)  2.28 us

profile of v6, /device:TPU:0, one launch (start us, length us, event | category | flops | bytes accessed | tf_op | source)
XLA Modules:
  0.0 109.0 jit_solution(13457429841198464822)
XLA Ops:
  0.0 0.7 convert_multiply_fusion
  0.7 0.9 compare_convert_fusion
  1.5 2.5 %copy.22 = bf16[128,16,256]{2,0,1:T(8,128)(2,1)} copy(bf16[128,16,256]{2,1,0:T(8,128)(2,1)} %tile_ref.1) | data formatting | bytes 2097152 | tf_op args[0]
  4.1 0.0 copy-start
  4.1 55.5 %transition.1 = (f32[8,256,256]{2,1,0:T(8,128)}, bf16[8,256,256]{2,1,0:T(8,128)(2,1)}, bf16[256,8,256]{2,1,0:T(8,128)(2,1)}) custom-call(bf16[128,16,256]{2,1,0:T(8,128)(2,1)} %tile_ref.1, bf16[16,128,256]{2,1,0:T(8,128)(2,1)} %bitcast.18, f32[1,256]{1,0:T(1,128)} %bitcast.21, bf16[256,1024]{1,0:T(8,128)(2,1)} %hidden_weight_ref.1, ...), custom_call_target="tpu_custom_call" | custom-call | tf_op jit(solution)/shard_map/transition/pallas_call | solution.py:639
  59.6 0.0 copy-done
  59.6 2.9 %fusion.1.bias_ref = f32[8,256,256]{2,1,0:T(8,128)} fusion(bf16[256,8,256]{2,1,0:T(8,128)(2,1)} %get-tuple-element.10, f32[256]{0:T(256)S(1)} %convert_multiply_fusion, f32[256,256]{1,0:T(8,128)S(1)} %compare_convert_fusion, f32[8]{0:T(128)S(1)} %copy-done), kind=kLoop, calls=%fused_computation.2 | loop fusion | flops 2621440 | bytes 3408928 | tf_op jit(solution)/shard_map/mul | solution.py:678
  62.5 44.2 %attention.1 = bf16[2,16,8,8,256]{4,3,2,1,0:T(8,128)(2,1)} custom-call(f32[8,256,256]{2,1,0:T(8,128)} %get-tuple-element.8.carried_ref, bf16[8,256,256]{2,1,0:T(8,128)(2,1)} %get-tuple-element.9.normed_ref, f32[8,256,256]{2,1,0:T(8,128)} %fusion.1.bias_ref, bf16[256,256]{1,0:T(8,128)(2,1)} %query_weight_ref.1, bf16[256,256]{1,0:T(8,128)(2,1)} %key_weight_ref.1, ...), custom_call_target="tpu_custom_call" | custom-call | tf_op jit(solution)/shard_map/attention/pallas_call | solution.py:683
  106.7 2.3 %copy.21 = bf16[128,2,8,256]{3,2,1,0:T(8,128)(2,1)} copy(bf16[128,2,8,256]{3,2,0,1:T(8,128)(2,1)} %bitcast.19) | data formatting | bytes 2097152 | tf_op jit(solution)/shard_map/transpose | solution.py:719
Async XLA Ops:
  4.1 55.5 %copy-start = (f32[8]{0:T(128)S(1)}, f32[8]{0:T(128)}, u32[]{:S(2)}) copy-start(f32[8]{0:T(128)} %param.26) | copy-start | bytes 100
